TPU v7x, 128 devices: a whole 4x4x4 slice. The times are simulated.
128 devices in a mesh: dp: 16 (over z_lo, x, core), group: 8 (over z_hi, y).
Axes of the slice: x: 4, y: 4, z: 4 (z_hi: 2, z_lo: 2; z = z_hi * 2 + z_lo), core: 2. Of those that a mesh axis runs over, the one named last changes fastest.
Arguments:
- activations: bfloat16 [2048, 8192], P('dp'), may hold values from -6 to 6
- out_grads: bfloat16 [2048, 28672], P('dp', 'group'), may hold values from -6 to 6
- basis_in: bfloat16 [16, 512, 512], P('dp'), may hold values from -0.25 to 0.25
- basis_out: bfloat16 [56, 512, 512], P('group'), may hold values from -0.25 to 0.25
- query_grads: bfloat16 [28672, 3, 8192], P('group', None, 'dp'), may hold values from -6 to 6
- eigenvalues: bfloat16 [28672, 8192], P('group', 'dp'), may hold values from 0.049804688 to 5
- doc_ids: int32 [2048], replicated, may hold values from 0 to 63, never falling along the last dimension, each value on 1 to 64 neighbouring positions
Outputs:
- doc_scores: float32 [3, 64], replicated
Inputs may be any that keep to these rules, and one draw needn't show every extreme that they name: doc_ids never falls along the tokens; every document 0 to 63 has 1 to 64 tokens, and one has exactly 64.
All inputs are finite; a program needn't handle non-finite values.
Results may differ from a plain program's by a relative error of at most 0.0055.
Values may be sent and summed in bfloat16 or wider, within the bound.
No kernel may reach another device: no remote copies, remote signals or barrier semaphores. Data moves between devices by JAX's collectives and lax.ppermute only.
A program may use at most 192 MiB of HBM per device.

v0:
```python
import math

import jax
import jax.numpy as jnp
from jax import lax
from jax.sharding import PartitionSpec as P

D = 8192
FF = 28672
DOC_AVG = 32


damping = 0.1


def rotate_rows(rows_in, basis):
    row_count = rows_in.shape[0]
    nblocks = basis.shape[0]
    block_width = basis.shape[1]
    shaped = rows_in.reshape(row_count, nblocks, block_width)
    turned = jnp.einsum("tnb,nbc->tnc", shaped, basis, preferred_element_type=jnp.float32)
    return turned.reshape(row_count, nblocks * block_width).astype(jnp.bfloat16)


def on_device(activations, out_grads, basis_in, basis_out, query_grads, eigenvalues, doc_ids):
    blocks_in = lax.all_to_all(activations, "dp", split_axis=1, concat_axis=0, tiled=True)
    rotated_in = rotate_rows(blocks_in, basis_in)
    out_cols = query_grads.shape[0]
    queries = query_grads.shape[1]
    in_cols = query_grads.shape[2]
    scaled = (
        query_grads.astype(jnp.float32) / (eigenvalues.astype(jnp.float32)[:, None, :] + damping)
    ).astype(jnp.bfloat16)
    scaled = scaled.reshape(out_cols, queries * in_cols)
    doc_total = doc_ids.shape[0] // DOC_AVG
    doc_range = jnp.arange(doc_total, dtype=jnp.int32)
    rotated_out = rotate_rows(out_grads, basis_out)
    grad_piece = lax.all_gather(rotated_out, "dp", axis=0, tiled=True)
    piece_rows = grad_piece.shape[0]
    projected = jnp.dot(grad_piece, scaled, preferred_element_type=jnp.float32).reshape(
        piece_rows, queries, in_cols
    )
    token_scores = jnp.sum(projected * rotated_in.astype(jnp.float32)[:, None, :], axis=2)
    membership = (doc_ids[:, None] == doc_range[None, :]).astype(jnp.float32)
    local_scores = jnp.dot(
        token_scores.T,
        membership,
        precision=lax.Precision.HIGHEST,
        preferred_element_type=jnp.float32,
    )
    doc_scores = lax.psum(local_scores, ("dp", "group"))
    return doc_scores * (1.0 / math.sqrt(FF * D))


def solution(mesh):
    return jax.shard_map(
        on_device,
        mesh=mesh,
        in_specs=(
            P("dp", None),
            P("dp", "group"),
            P("dp", None, None),
            P("group", None, None),
            P("group", None, "dp"),
            P("group", "dp"),
            P(),
        ),
        out_specs=P(),
        check_vma=False,
    )
```

profile of v0, /device:TPU:1, one launch (start us, length us, event | category | flops | bytes accessed | tf_op | source)
XLA Modules:
  0.0 226.4 jit_solution(9948356858457873738)
XLA Ops:
  6.5 0.0 copy-start
  6.5 0.0 all-gather.2.cloned.1.call-start
  6.5 1.6 copy.25
  8.2 3.3 %convolution_convert_fusion.1 = bf16[7,512,128]{2,1,0:T(8,128)(2,1)S(1)} fusion(bf16[7,512,512]{2,1,0:T(8,128)(2,1)} %param.10, bf16[128,7,512]{0,2,1:T(8,128)(2,1)S(1)} %bitcast.40), kind=kOutput, calls=%fused_computation.10 | convolution fusion | flops 470220800 | bytes 5505024 | tf_op jit(solution)/shard_map/tnb,nbc->tnc/dot_general | solution.py:21
  11.5 1.3 copy.28
  12.8 0.0 all-gather.2.cloned.1.call-update
  12.8 4.1 %copy.31 = bf16[128,8192]{0,1:T(8,128)(2,1)} copy(bf16[128,8192]{1,0:T(8,128)(2,1)} %param.7) | data formatting | bytes 4194304 | tf_op args[0]
  16.9 7.2 %all-to-all-start = ((bf16[128,16,512]{0,2,1:T(8,128)(2,1)}), bf16[128,16,512]{0,2,1:T(8,128)(2,1)S(1)}, u32[]{:S(2)}, u32[]{:S(2)}) async-start(bf16[128,16,512]{0,2,1:T(8,128)(2,1)} %bitcast.38), calls=%async_computation | async-start | bytes 4194304 | tf_op jit(solution)/shard_map/all_to_all | solution.py:26
  24.1 6.4 %convert_add_fusion = f32[3584,512]{1,0:T(8,128)} fusion(bf16[3584,512]{1,0:T(8,128)(2,1)} %param.12), kind=kLoop, calls=%fused_computation.6 | loop fusion | flops 3670016 | bytes 11010048 | tf_op jit(solution)/shard_map/add | solution.py:32
  30.5 8.4 %copy.30 = f32[3584,512]{0,1:T(8,128)} copy(f32[3584,512]{1,0:T(8,128)} %convert_add_fusion) | data formatting | bytes 14680064 | tf_op jit(solution)/shard_map/add | solution.py:32
  38.9 14.7 %copy.29 = bf16[3584,3,512]{0,2,1:T(8,128)(2,1)} copy(bf16[3584,3,512]{2,0,1:T(8,128)(2,1)} %param.11) | data formatting | bytes 22020096 | tf_op args[4]
  53.6 18.2 %all-to-all-done = bf16[128,16,512]{0,2,1:T(8,128)(2,1)S(1)} async-done(((bf16[128,16,512]{0,2,1:T(8,128)(2,1)}), bf16[128,16,512]{0,2,1:T(8,128)(2,1)S(1)}, u32[]{:S(2)}, u32[]{:S(2)}) %all-to-all-start) | async-done | bytes 2097184 | tf_op jit(solution)/shard_map/all_to_all | solution.py:26
  71.8 2.6 %copy.32 = bf16[16,128,512]{2,1,0:T(8,128)(2,1)} copy(bf16[16,128,512]{1,2,0:T(8,128)(2,1)S(1)} %bitcast.37) | data formatting | bytes 4194304 | tf_op jit(solution)/shard_map/all_to_all | solution.py:26
  74.4 0.0 copy-done
  74.4 4.9 %convert_bitcast_fusion = f32[2048,512]{0,1:T(8,128)} fusion(bf16[2048,512]{1,0:T(8,128)(2,1)} %bitcast.41, bf16[1,512,512]{2,1,0:T(8,128)(2,1)S(1)} %copy-done), kind=kOutput, calls=%fused_computation.7 | convolution fusion | flops 1075838976 | bytes 6815744 | tf_op jit(solution)/shard_map/tnb,nbc->tnc/dot_general | solution.py:21
  79.4 0.0 copy-start.2
  79.4 40.7 %all-gather.2.cloned.1.call-done = bf16[2048,3584]{1,0:T(8,128)(2,1)} async-done(((bf16[128,3584]{1,0:T(8,128)(2,1)}), bf16[2048,3584]{1,0:T(8,128)(2,1)}) %all-gather.2.cloned.1.call-update) | async-done | bytes 14680080 | tf_op jit(solution)/shard_map/all_gather | solution.py:38
  120.1 0.0 copy-start.1
  120.1 31.9 %multiply_reduce_fusion = f32[2048,3]{0,1:T(4,128)S(1)} fusion(f32[2048,512]{0,1:T(8,128)} %convert_bitcast_fusion, bf16[3584,3,512]{0,2,1:T(8,128)(2,1)} %copy.29, f32[3584,512]{0,1:T(8,128)} %copy.30, bf16[2048,3584]{1,0:T(8,128)(2,1)} %all-gather.2.cloned.1.call-done), kind=kOutput, calls=%fused_computation.3 | convolution fusion | flops 22571378688 | bytes 37249024 | tf_op jit(solution)/shard_map/dot_general | solution.py:40
  152.0 0.0 copy-done.2
  152.0 0.6 fusion.10
  152.6 66.3 %psum.7 = f32[3,64]{1,0:T(4,128)S(1)} all-reduce(f32[3,64]{1,0:T(4,128)S(1)} %fusion.10), channel_id=1, replica_groups=mesh['dp'=16,'group'=8] {'dp','group'}, use_global_device_ids=true, to_apply=%region_1.0 | all-reduce | flops 192 | bytes 1536 | tf_op jit(solution)/shard_map/psum | solution.py:51
  218.9 0.6 broadcast_multiply_fusion
  219.5 0.0 copy-done.1
Async XLA Ops:
  6.5 67.9 %copy-start = (bf16[1,512,512]{2,1,0:T(8,128)(2,1)S(1)}, bf16[1,512,512]{2,1,0:T(8,128)(2,1)}, u32[]{:S(2)}) copy-start(bf16[1,512,512]{2,1,0:T(8,128)(2,1)} %param.9) | copy-start | bytes 1572868
  6.5 113.6 %all-gather.2.cloned.1.call-start = ((), (), s32[]{:S(2)}) async-start(), calls=%async_computation.1 | async-start | bytes 15597568 | tf_op jit(solution)/shard_map/all_gather | solution.py:38
  16.9 54.9 %all-to-all-start = ((bf16[128,16,512]{0,2,1:T(8,128)(2,1)}), bf16[128,16,512]{0,2,1:T(8,128)(2,1)S(1)}, u32[]{:S(2)}, u32[]{:S(2)}) async-start(bf16[128,16,512]{0,2,1:T(8,128)(2,1)} %bitcast.38), calls=%async_computation | async-start | bytes 4194304 | tf_op jit(solution)/shard_map/all_to_all | solution.py:26
  79.4 72.7 %copy-start.2 = (s32[2048]{0:T(1024)S(1)}, s32[2048]{0:T(1024)}, u32[]{:S(2)}) copy-start(s32[2048]{0:T(1024)} %param.13) | copy-start | bytes 24580
  120.1 99.4 %copy-start.1 = (bf16[1,512,512]{2,1,0:T(8,128)(2,1)S(1)}, bf16[1,512,512]{2,1,0:T(8,128)(2,1)}, u32[]{:S(2)}) copy-start(bf16[1,512,512]{2,1,0:T(8,128)(2,1)} %param.9) | copy-start | bytes 1572868
Sparse Core Ops, SparseCore 0:
  12.9 107.1 all-gather.1
where the time goes:
time: 227 us; the launch traced here: 226 us
  blocking collectives  66.3 us (29%)
  waiting for transfers between devices  58.9 us (26%)
  matrix products  40.7 us (18%)
  local copies, waits for them, and re-layouts  32.8 us (14%)
  between operations  13.4 us (6%)
  starting transfers between devices  7.16 us (3%)
  other arithmetic  6.97 us (3%)
    psum x1, blocking collectives, on_device(): doc_scores = lax.psum(local_scores, ('dp', 'group'))  66.3 us
    all_gather x1, waiting for transfers between devices, on_device(): grad_piece = lax.all_gather(rotated_out, 'dp', axis=0, tiled=True)  40.7 us
    dot_general x1, matrix products, on_device(): jnp.dot(grad_piece, scaled, preferred_element_type=jnp.float32)  31.9 us
    unnamed x9, local copies, waits for them, and re-layouts  20.4 us
    all_to_all x1, waiting for transfers between devices, on_device(): lax.all_to_all(activations, 'dp', split_axis=1, concat_axis=0, tiled=True)  18.2 us
    add x1, local copies, waits for them, and re-layouts, on_device(): eigenvalues.astype(jnp.float32)[:, None, :] + damping  8.43 us
    dot_general x2, matrix products, rotate_rows(): jnp.einsum('tnb,nbc->tnc', shaped, basis, preferred_element_type=jnp.floa...  8.25 us
    all_to_all x1, starting transfers between devices, on_device(): lax.all_to_all(activations, 'dp', split_axis=1, concat_axis=0, tiled=True)  7.16 us
  transfers between devices with their start and end apart: 2, of which 2 were waited for; matrix products, arithmetic and copies ran while one was open for 18% of the time, Pallas kernels for 0%

commit v1 on v0

v1 whole, which is shorter than its diff:
```python
import functools
import math

import jax
import jax.numpy as jnp
from jax import lax
from jax.experimental import pallas as pl
from jax.experimental.pallas import tpu as pltpu
from jax.sharding import PartitionSpec as P


D = 8192
FF = 28672
DOCS = 64
BLK = 512
ROWS = 128
Q = 3
damping = 0.1


HIGHEST = lax.Precision.HIGHEST
F32 = jnp.float32
BF16 = jnp.bfloat16


def dp_perm(dz, dx, dc):
    pairs = []
    for i in range(16):
        z, x, c = i // 8, (i // 2) % 4, i % 2
        pairs.append((i, (((z + dz) % 2) * 4 + (x + dx) % 4) * 2 + (c + dc) % 2))
    return pairs


def y_perm(dy):
    return [(g, (g // 4) * 4 + (g + dy) % 4) for g in range(8)]


RIGHT, LEFT, ACROSS, MATE = dp_perm(0, 1, 0), dp_perm(0, -1, 0), dp_perm(1, 0, 0), dp_perm(0, 0, 1)

STEP1 = ((0, 3), (0, 1), (1, 0))
STEP2 = ((0, 2), (1, 1), (1, 3))
ORDER = (
    ((0, 0, 0), (0, 0, 1))
    + tuple((z, x, c) for c in (0, 1) for z, x in STEP1)
    + tuple((z, x, c) for c in (0, 1) for z, x in STEP2)
    + ((1, 2, 0), (1, 2, 1))
)


def source(dp, offset):
    dz, dx, dc = offset
    z, x, c = dp // 8, (dp // 2) % 4, dp % 2
    return (((z + dz) % 2) * 4 + (x + dx) % 4) * 2 + (c + dc) % 2


def cut_kernel(y_ref, rows_ref, out_ref):
    for d in range(out_ref.shape[0]):
        out_ref[d] = rows_ref[:, d * BLK:(d + 1) * BLK]


def cut(activations, y):
    quarter = ROWS // 4
    return pl.pallas_call(
        cut_kernel,
        out_shape=jax.ShapeDtypeStruct((16, quarter, BLK), BF16),
        grid_spec=pltpu.PrefetchScalarGridSpec(
            num_scalar_prefetch=1,
            grid=(1,),
            in_specs=[pl.BlockSpec((quarter, D), lambda i, y: (y[0], 0))],
            out_specs=pl.BlockSpec((16, quarter, BLK), lambda i, y: (0, 0, 0)),
        ),
        cost_estimate=pl.CostEstimate(flops=0, bytes_accessed=1 << 20, transcendentals=0),
        name="cut",
    )(y, activations)


def turn_kernel(dp_ref, rows_ref, basis_ref, out_ref, gathered):
    dp = dp_ref[0]
    quarter = rows_ref.shape[1]
    for k, offset in enumerate(ORDER):
        gathered[k * quarter:(k + 1) * quarter] = rows_ref[source(dp, offset)]
    turned = jnp.dot(gathered[...], basis_ref[0], preferred_element_type=F32).astype(BF16)
    out_ref[...] = turned.reshape(16, quarter, BLK)


def turn(dp, rows, basis):
    quarter = rows.shape[1]
    return pl.pallas_call(
        turn_kernel,
        out_shape=jax.ShapeDtypeStruct((16, quarter, BLK), BF16),
        grid_spec=pltpu.PrefetchScalarGridSpec(
            num_scalar_prefetch=1,
            grid=(1,),
            in_specs=[
                pl.BlockSpec((16, quarter, BLK), lambda i, d: (0, 0, 0)),
                pl.BlockSpec((1, BLK, BLK), lambda i, d: (0, 0, 0)),
            ],
            out_specs=pl.BlockSpec((16, quarter, BLK), lambda i, d: (0, 0, 0)),
            scratch_shapes=[pltpu.VMEM((16 * quarter, BLK), BF16)],
        ),
        cost_estimate=pl.CostEstimate(flops=10**10, bytes_accessed=3 << 19, transcendentals=0),
        compiler_params=pltpu.CompilerParams(vmem_limit_bytes=8 << 20),
        name="turn",
    )(dp, rows, basis)


def folded(basis_ref, query_ref, eigen_ref):
    inverse = 1.0 / (eigen_ref[...].astype(F32) + damping)
    for q in range(Q):
        scaled = (query_ref[q].astype(F32) * inverse).astype(BF16)
        yield q, jnp.dot(basis_ref[0], scaled, preferred_element_type=F32).astype(BF16)


def fold_specs(first):
    return [
        pl.BlockSpec((1, BLK, BLK), lambda b: (first + b, 0, 0)),
        pl.BlockSpec((Q, BLK, BLK), lambda b: (0, first + b, 0)),
        pl.BlockSpec((BLK, BLK), lambda b: (first + b, 0)),
    ]


def fold_cost(nblocks):
    return pl.CostEstimate(
        flops=2 * Q * nblocks * BLK**3, bytes_accessed=nblocks << 22, transcendentals=0
    )


def early_kernel(basis_ref, query_ref, eigen_ref, out_ref):
    for q, values in folded(basis_ref, query_ref, eigen_ref):
        out_ref[q] = values


def fold_early(nblocks, basis_out, query, eigenvalues):
    return pl.pallas_call(
        early_kernel,
        out_shape=jax.ShapeDtypeStruct((Q, nblocks * BLK, BLK), BF16),
        grid=(nblocks,),
        in_specs=fold_specs(0),
        out_specs=pl.BlockSpec((Q, BLK, BLK), lambda b: (0, b, 0)),
        cost_estimate=fold_cost(nblocks),
        name="early",
    )(distant(basis_out), distant(query), distant(eigenvalues))


TILE = 256
WHOLE = pl.BlockSpec(memory_space=pltpu.VMEM)
SCALARS = pl.BlockSpec(memory_space=pltpu.SMEM)
distant = lambda v: pltpu.with_memory_space_constraint(v, pltpu.HBM)
resident = lambda v: pltpu.with_memory_space_constraint(v, pltpu.VMEM)


def product_kernel(*refs):
    row_refs, (weight_ref, out_ref) = refs[:-2], refs[-2:]

    def body(q, carry):
        for part in range(BLK // TILE):
            rows = jnp.concatenate([ref[...] for ref in row_refs], axis=0)
            tile = weight_ref[q, :, part * TILE:(part + 1) * TILE]
            out_ref[q, :, part * TILE:(part + 1) * TILE] = jnp.dot(rows, tile, preferred_element_type=F32)
        return carry

    lax.fori_loop(0, Q, body, 0)


def product(rows, weight):
    height = sum(r.shape[0] for r in rows)
    depth = weight.shape[1]
    return pl.pallas_call(
        product_kernel,
        out_shape=pltpu.VMEM((Q, height, BLK), F32),
        in_specs=[WHOLE] * (len(rows) + 1),
        out_specs=WHOLE,
        cost_estimate=pl.CostEstimate(
            flops=2 * height * depth * Q * BLK, bytes_accessed=0, transcendentals=0
        ),
        compiler_params=pltpu.CompilerParams(vmem_limit_bytes=8 << 20),
    )(*[resident(r) for r in rows], resident(weight))


def place(inputs, pieces, y, first):
    quarter = ROWS // 4
    for k in range(inputs.shape[0] // ROWS):
        for shift, piece in enumerate(pieces):
            start = pl.multiple_of(k * ROWS + ((y + shift) % 4) * quarter, quarter)
            inputs[pl.ds(start, quarter), :] = piece[first + k]


def narrowed(values):
    return sum([values[:, i:i + 128] for i in range(128, values.shape[1], 128)], values[:, :128])


def doc_sums(dp, offsets, ids_ref, tokens, before):
    docs = lax.broadcasted_iota(jnp.int32, (DOCS, ROWS), 0)
    member = jnp.concatenate(
        [(docs == ids_ref[source(dp, offset)]).astype(F32) for offset in offsets], axis=1
    )
    return [
        before[q] + jnp.dot(member, tokens[q], precision=HIGHEST, preferred_element_type=F32) for q in range(Q)
    ]


def settle_kernel(offsets, first, counts, pos_ref, r0, r1, r2, r3, ids_ref, *refs):
    projected, (out_ref, inputs, tokens) = refs[:-3], refs[-3:]
    dp, y = pos_ref[0], pos_ref[1]
    place(inputs, (r0, r1, r2, r3), y, first)

    def body(q, carry):
        start = 0
        for ref, count in zip(projected, counts):
            for k in range(count):
                values = ref[q, k * ROWS:(k + 1) * ROWS, :] * inputs[start:start + ROWS, :].astype(F32)
                tokens[q, start:start + ROWS] = narrowed(values)
                start += ROWS
        return carry

    lax.fori_loop(0, Q, body, 0)
    for q, sums in enumerate(doc_sums(dp, offsets, ids_ref, tokens, (0.0,) * Q)):
        out_ref[q] = sums


def settle(position, projected, offsets, first, pieces, ids):
    counts = tuple(p.shape[1] // ROWS for p in projected)
    height = len(offsets) * ROWS
    return pl.pallas_call(
        functools.partial(settle_kernel, offsets, first, counts),
        out_shape=jax.ShapeDtypeStruct((Q, DOCS, 128), F32),
        in_specs=[SCALARS] + [WHOLE] * (5 + len(projected)),
        out_specs=WHOLE,
        scratch_shapes=[pltpu.VMEM((height, BLK), BF16), pltpu.VMEM((Q, height, 128), F32)],
        cost_estimate=pl.CostEstimate(
            flops=2 * height * Q * BLK, bytes_accessed=8 << 20, transcendentals=0
        ),
        compiler_params=pltpu.CompilerParams(vmem_limit_bytes=8 << 20),
    )(position, *[resident(p) for p in pieces], resident(ids), *[resident(p) for p in projected])


def score_kernel(offsets, first, last, pos_ref, *refs):
    row_refs, refs = refs[:-10], refs[-10:]
    weight_ref, r0, r1, r2, r3, ids_ref, before_ref, out_ref, inputs, tokens = refs
    dp, y = pos_ref[0], pos_ref[1]
    place(inputs, (r0, r1, r2, r3), y, first)

    def body(q, carry):
        for part in range(BLK // TILE):
            columns = slice(part * TILE, (part + 1) * TILE)
            rows = jnp.concatenate([ref[...] for ref in row_refs], axis=0)
            values = jnp.dot(rows, weight_ref[q, :, columns], preferred_element_type=F32)
            narrow = narrowed(values * inputs[:, columns].astype(F32))
            if part == 0:
                tokens[q] = narrow
            else:
                tokens[q] += narrow
        return carry

    lax.fori_loop(0, Q, body, 0)
    sums = doc_sums(dp, offsets, ids_ref, tokens, [before_ref[q] for q in range(Q)])
    if last:
        flat = lax.dot_general(
            jnp.ones((8, 128), F32),
            jnp.concatenate(sums, axis=0),
            (((1,), (1,)), ((), ())),
            precision=HIGHEST,
            preferred_element_type=F32,
        )
        out_ref[...] = jnp.broadcast_to(flat[None, :1], out_ref.shape)
    else:
        for q in range(Q):
            out_ref[q] = sums[q]


def score(position, rows, offsets, first, weight, pieces, ids, before, last=False):
    height = len(offsets) * ROWS
    depth = weight.shape[1]
    out = (128, 1, Q * DOCS) if last else (Q, DOCS, 128)
    return pl.pallas_call(
        functools.partial(score_kernel, offsets, first, last),
        out_shape=jax.ShapeDtypeStruct(out, F32),
        in_specs=[SCALARS] + [WHOLE] * (len(rows) + 7),
        out_specs=WHOLE,
        scratch_shapes=[pltpu.VMEM((height, BLK), BF16), pltpu.VMEM((Q, height, 128), F32)],
        cost_estimate=pl.CostEstimate(
            flops=2 * height * depth * Q * BLK, bytes_accessed=0, transcendentals=0
        ),
        compiler_params=pltpu.CompilerParams(vmem_limit_bytes=8 << 20),
    )(
        position,
        *[resident(r) for r in rows],
        resident(weight),
        *[resident(p) for p in pieces],
        resident(ids),
        resident(before),
    )


def finish_kernel(parts_ref, out_ref):
    total = jnp.sum(parts_ref[...], axis=0) * (1.0 / math.sqrt(FF * D))
    for q in range(Q):
        out_ref[q:q + 1, :] = total[:, q * DOCS:(q + 1) * DOCS]


def move(v, perm, axis="dp"):
    return lax.ppermute(v, axis, perm)


def on_device(activations, out_grads, basis_in, basis_out, query_grads, eigenvalues, doc_ids):
    dp = lax.axis_index("dp")
    y = lax.axis_index("group") % 4
    position = jnp.stack([dp, y]).astype(jnp.int32)
    ids = doc_ids.reshape(16, 1, ROWS)

    a3 = move(out_grads, RIGHT)
    b0 = move(out_grads, ACROSS)
    a1 = move(out_grads, LEFT)
    mate = move(out_grads, MATE)

    columns = lax.all_to_all(cut(activations, position[1:]), "dp", 0, 0, tiled=True)
    turned = turn(position[:1], columns, basis_in)
    pieces = [turned] + [move(turned, y_perm(-k), "group") for k in (1, 3, 2)]
    pieces = [pieces[0], pieces[1], pieces[3], pieces[2]]

    query = jnp.transpose(query_grads, (1, 0, 2))
    weight = fold_early(7, basis_out, query, eigenvalues)

    a2 = move(a3, RIGHT)
    b3 = move(a3, ACROSS)
    b1 = move(b0, LEFT)
    step1 = [move(v, MATE) for v in (a3, a1, b0)]
    parts = [move(b3[:48], RIGHT), move(b1[48:80], LEFT), move(a2[80:], ACROSS)]
    step2 = [move(v, MATE) for v in (a2, b1, b3)]
    step3 = [move(v, MATE) for v in parts]

    projected = [product([out_grads, mate, a3, a1, b0], weight), product(step1, weight)]
    projected.append(product([a2, b1, b3], weight))
    total = settle(position, projected, ORDER[:11], 0, pieces, ids)
    total = score(position, step2, ORDER[11:14], 11, weight, pieces, ids, total)
    partial = score(position, parts + step3, ORDER[14:], 14, weight, pieces, ids, total, True)

    partials = lax.all_to_all(partial, ("dp", "group"), 0, 0, tiled=True)
    return pl.pallas_call(
        finish_kernel,
        out_shape=jax.ShapeDtypeStruct((Q, DOCS), F32),
        in_specs=[WHOLE],
        out_specs=WHOLE,
        compiler_params=pltpu.CompilerParams(vmem_limit_bytes=4 << 20),
        name="finish",
    )(resident(partials))


def solution(mesh):
    return jax.shard_map(
        on_device,
        mesh=mesh,
        in_specs=(
            P("dp", None),
            P("dp", "group"),
            P("dp", None, None),
            P("group", None, None),
            P("group", None, "dp"),
            P("group", "dp"),
            P(),
        ),
        out_specs=P(),
        check_vma=False,
    )
```

time: 227 us -> 147 us (0.65)
  Pallas kernels: 0 us -> 54.3 us
  blocking collectives: 66.3 us -> 17.2 us
  matrix products: 40.7 us -> 0 us
  local copies, waits for them, and re-layouts: 32.8 us -> 6.12 us
  starting transfers between devices: 7.16 us -> 31.3 us
  waiting for transfers between devices: 58.9 us -> 37.1 us
  between operations: 13.4 us -> 0.16 us
  other arithmetic: 6.97 us -> 0.07 us
    psum x1 -> x0, blocking collectives: 66.3 us -> none  [on_device(): doc_scores = lax.psum(local_scores, ('dp', 'group'))]
    pallas_call x0 -> x10, Pallas kernels: none -> 54.3 us  [the longest x3 22.4 us: product(): pl.pallas_call(product_kernel, out_shape=pltpu.VMEM((Q, height, BLK), F32...]
    dot_general x4 -> x0, matrix products: 40.7 us -> none  [the longest x1 31.9 us: on_device(): jnp.dot(grad_piece, scaled, preferred_element_type=jnp.float32)]
    all_gather x1 -> x0, waiting for transfers between devices: 40.7 us -> none  [on_device(): grad_piece = lax.all_gather(rotated_out, 'dp', axis=0, tiled=True)]
    ppermute x0 -> x22, waiting for transfers between devices: none -> 32.9 us  [move(): return lax.ppermute(v, axis, perm)]
    ppermute x0 -> x22, starting transfers between devices: none -> 24.1 us  [move(): return lax.ppermute(v, axis, perm)]
    all_to_all x0 -> x1, blocking collectives: none -> 17.2 us  [on_device(): partials = lax.all_to_all(partial, ('dp', 'group'), 0, 0, tiled=True)]
    unnamed x9 -> x8, local copies, waits for them, and re-layouts: 20.4 us -> 4.14 us
  transfers between devices with their start and end apart: 2 -> 23, of which waited for: 2 -> 4; matrix products, arithmetic and copies ran while one was open for 18% -> 1% of each run, Pallas kernels for 0% -> 32%
where the time goes in v1:
time: 147 us; the launch traced here: 146 us
  Pallas kernels  54.3 us (37%)
  waiting for transfers between devices  37.1 us (25%)
  starting transfers between devices  31.3 us (21%)
  blocking collectives  17.2 us (12%)
  local copies, waits for them, and re-layouts  6.12 us (4%)
    ppermute x22, waiting for transfers between devices, move(): return lax.ppermute(v, axis, perm)  32.9 us
    ppermute x22, starting transfers between devices, move(): return lax.ppermute(v, axis, perm)  24.1 us
    pallas_call x3, Pallas kernels, product(): pl.pallas_call(product_kernel, out_shape=pltpu.VMEM((Q, height, BLK), F32...  22.4 us
    all_to_all x1, blocking collectives, on_device(): partials = lax.all_to_all(partial, ('dp', 'group'), 0, 0, tiled=True)  17.2 us
    pallas_call x1, Pallas kernels, fold_early(): pl.pallas_call(early_kernel, out_shape=jax.ShapeDtypeStruct((Q, nblocks *...  15.5 us
    pallas_call x2, Pallas kernels, score(): pl.pallas_call(functools.partial(score_kernel, offsets, first, last), out...  10.3 us
    all_to_all x1, starting transfers between devices, on_device(): lax.all_to_all(cut(activations, position[1:]), 'dp', 0, 0, tiled=True)  7.16 us
    all_to_all x1, waiting for transfers between devices, on_device(): lax.all_to_all(cut(activations, position[1:]), 'dp', 0, 0, tiled=True)  4.23 us
  transfers between devices with their start and end apart: 23, of which 4 were waited for; matrix products, arithmetic and copies ran while one was open for 1% of the time, Pallas kernels for 32%

profile of v1, /device:TPU:1, one launch (start us, length us, event | category | flops | bytes accessed | tf_op | source)
XLA Modules:
  0.0 146.2 jit_solution(13352256727567707214)
XLA Ops:
  0.0 1.9 %cut.1 = bf16[16,32,512]{2,1,0:T(8,128)(2,1)} custom-call(s32[1]{0:T(128)} %bitcast.1.y_ref, bf16[128,8192]{1,0:T(8,128)(2,1)} %rows_ref.1), custom_call_target="tpu_custom_call" | custom-call | bytes 1048576 | tf_op jit(solution)/shard_map/cut/pallas_call | solution.py:63
  1.9 7.2 %all-to-all-start = ((bf16[16,32,512]{2,1,0:T(8,128)(2,1)}), bf16[16,32,512]{2,1,0:T(8,128)(2,1)S(1)}, u32[]{:S(2)}, u32[]{:S(2)}) async-start(bf16[16,32,512]{2,1,0:T(8,128)(2,1)} %cut.1), calls=%async_computation | async-start | bytes 1048576 | tf_op jit(solution)/shard_map/all_to_all | solution.py:316
  9.1 1.4 collective-permute-start
  10.5 1.2 collective-permute-start.3
  11.6 1.5 %collective-permute-start.18 = (bf16[128,3584]{1,0:T(8,128)(2,1)}, bf16[128,3584]{1,0:T(8,128)(2,1)}, u32[]{:S(2)}, u32[]{:S(2)}) collective-permute-start(bf16[128,3584]{1,0:T(8,128)(2,1)} %refs_0_.1), channel_id=1, source_target_pairs={{0,48},{8,56},{16,0},{24,8},{32,16},{40,24},{48,32},{56,40},{64,11... | collective-permute-start | bytes 2752520 | tf_op jit(solution)/shard_map/ppermute | solution.py:302
  13.1 1.2 collective-permute-start.17
  14.4 4.2 %all-to-all-done.rows_ref = bf16[16,32,512]{2,1,0:T(8,128)(2,1)S(1)} async-done(((bf16[16,32,512]{2,1,0:T(8,128)(2,1)}), bf16[16,32,512]{2,1,0:T(8,128)(2,1)S(1)}, u32[]{:S(2)}, u32[]{:S(2)}) %all-to-all-start) | async-done | bytes 524320 | tf_op jit(solution)/shard_map/all_to_all | solution.py:316
  18.6 0.4 turn.1.r0.refs_4_.refs_7_
  19.1 2.8 %collective-permute-start.11 = (bf16[16,32,512]{2,1,0:T(8,128)(2,1)S(1)}, bf16[16,32,512]{2,1,0:T(8,128)(2,1)S(1)}, u32[]{:S(2)}, u32[]{:S(2)}) collective-permute-start(bf16[16,32,512]{2,1,0:T(8,128)(2,1)S(1)} %turn.1.r0.refs_4_.refs_7_), channel_id=1, source_target_pairs={{0,3},{1,0},{2,1},{3,2},{4,7},{5,4},{6,5},{7,6},{8,11},{9,8},{10,9... | collective-permute-start | bytes 1572872 | tf_op jit(solution)/shard_map/ppermute | solution.py:302
  21.9 16.3 %collective-permute-done.refs_2_ = bf16[128,3584]{1,0:T(8,128)(2,1)} collective-permute-done((bf16[128,3584]{1,0:T(8,128)(2,1)}, bf16[128,3584]{1,0:T(8,128)(2,1)}, u32[]{:S(2)}, u32[]{:S(2)}) %collective-permute-start) | collective-permute-done | bytes 917536 | tf_op jit(solution)/shard_map/ppermute | solution.py:302
  38.1 2.9 %collective-permute-start.12 = (bf16[16,32,512]{2,1,0:T(8,128)(2,1)S(1)}, bf16[16,32,512]{2,1,0:T(8,128)(2,1)S(1)}, u32[]{:S(2)}, u32[]{:S(2)}) collective-permute-start(bf16[16,32,512]{2,1,0:T(8,128)(2,1)S(1)} %turn.1.r0.refs_4_.refs_7_), channel_id=1, source_target_pairs={{0,2},{1,3},{2,0},{3,1},{4,6},{5,7},{6,4},{7,5},{8,10},{9,11},{10,... | collective-permute-start | bytes 1572872 | tf_op jit(solution)/shard_map/ppermute | solution.py:302
  41.4 1.2 collective-permute-start.1
  42.6 2.7 %collective-permute-start.4 = (bf16[128,3584]{1,0:T(8,128)(2,1)}, bf16[128,3584]{1,0:T(8,128)(2,1)}, u32[]{:S(2)}, u32[]{:S(2)}) collective-permute-start(bf16[128,3584]{1,0:T(8,128)(2,1)} %collective-permute-done.3.refs_4_), channel_id=1, source_target_pairs={{0,48},{8,56},{16,0},{24,8},{32,16},{40,24},{48,32},{56,40},{64,11... | collective-permute-start | bytes 2752520 | tf_op jit(solution)/shard_map/ppermute | solution.py:302
  45.3 7.0 %collective-permute-done.12.r2.refs_6_.refs_9_ = bf16[16,32,512]{2,1,0:T(8,128)(2,1)S(1)} collective-permute-done((bf16[16,32,512]{2,1,0:T(8,128)(2,1)S(1)}, bf16[16,32,512]{2,1,0:T(8,128)(2,1)S(1)}, u32[]{:S(2)}, u32[]{:S(2)}) %collective-permute-start.12) | collective-permute-done | bytes 524320 | tf_op jit(solution)/shard_map/ppermute | solution.py:302
  52.4 2.9 %collective-permute-start.19 = (bf16[128,3584]{1,0:T(8,128)(2,1)}, bf16[128,3584]{1,0:T(8,128)(2,1)}, u32[]{:S(2)}, u32[]{:S(2)}) collective-permute-start(bf16[128,3584]{1,0:T(8,128)(2,1)} %collective-permute-done.refs_2_), channel_id=1, source_target_pairs={{0,8},{8,0},{16,24},{24,16},{32,40},{40,32},{48,56},{56,48},{64,72... | collective-permute-start | bytes 2752520 | tf_op jit(solution)/shard_map/ppermute | solution.py:302
  55.2 9.6 %collective-permute-done.13.r3.refs_7_.refs_10_ = bf16[16,32,512]{2,1,0:T(8,128)(2,1)S(1)} collective-permute-done((bf16[16,32,512]{2,1,0:T(8,128)(2,1)S(1)}, bf16[16,32,512]{2,1,0:T(8,128)(2,1)S(1)}, u32[]{:S(2)}, u32[]{:S(2)}) %collective-permute-start.13) | collective-permute-done | bytes 524320 | tf_op jit(solution)/shard_map/ppermute | solution.py:302
  65.2 15.5 %early.1.refs_5_.refs_3_.refs_6_ = bf16[3,3584,512]{2,1,0:T(8,128)(2,1)} custom-call(bf16[7,512,512]{2,1,0:T(8,128)(2,1)} %basis_ref.2, bf16[3,3584,512]{2,1,0:T(8,128)(2,1)} %bitcast.7, bf16[3584,512]{1,0:T(8,128)(2,1)} %eigen_ref.1), custom_call_target="tpu_custom_call" | custom-call | flops 5637144576 | bytes 29360128 | tf_op jit(solution)/shard_map/early/pallas_call | solution.py:134
  81.8 4.1 %copy-done = bf16[3,3584,512]{2,1,0:T(8,128)(2,1)S(1)} copy-done((bf16[3,3584,512]{2,1,0:T(8,128)(2,1)S(1)}, bf16[3,3584,512]{2,1,0:T(8,128)(2,1)}, u32[]{:S(2)}) %copy-start) | copy-done | bytes 11010072
  86.0 10.0 %shard_map.73.refs_0_ = f32[3,640,512]{2,1,0:T(8,128)S(1)} custom-call(bf16[128,3584]{1,0:T(8,128)(2,1)} %refs_0_.1, bf16[128,3584]{1,0:T(8,128)(2,1)} %collective-permute-done.17.refs_1_, bf16[128,3584]{1,0:T(8,128)(2,1)} %collective-permute-done.refs_2_, bf16[128,3584]{1,0:T(8,128)(2,1)} %collective-permute-done.18.refs_3_, ...), custom_call_target="tpu_custom_call" | custom-call | flops 7046430720 | tf_op jit(solution)/shard_map/pallas_call | solution.py:168
  96.0 1.0 slice.14
  97.0 1.0 slice.13
  98.0 0.5 collective-permute-start.5
  98.5 6.2 %shard_map.75.refs_2_ = f32[3,384,512]{2,1,0:T(8,128)S(1)} custom-call(bf16[128,3584]{1,0:T(8,128)(2,1)} %collective-permute-done.6.refs_0_, bf16[128,3584]{1,0:T(8,128)(2,1)} %collective-permute-done.4.refs_1_, bf16[128,3584]{1,0:T(8,128)(2,1)S(1)} %collective-permute-done.1.refs_2_, bf16[3,3584,512]{2,1,0:T(8,128)(2,1)S(1)} %copy-done.1), custom_call_target="tpu_custom_call" | custom-call | flops 4227858432 | tf_op jit(solution)/shard_map/pallas_call | solution.py:168
  104.7 1.3 collective-permute-start.7
  106.0 1.1 collective-permute-start.2
  107.0 6.2 %shard_map.74.refs_1_ = f32[3,384,512]{2,1,0:T(8,128)S(1)} custom-call(bf16[128,3584]{1,0:T(8,128)(2,1)} %collective-permute-done.19.refs_0_, bf16[128,3584]{1,0:T(8,128)(2,1)S(1)} %collective-permute-done.20.refs_1_, bf16[128,3584]{1,0:T(8,128)(2,1)} %collective-permute-done.21.refs_2_, bf16[3,3584,512]{2,1,0:T(8,128)(2,1)S(1)} %copy-done.1), custom_call_target="tpu_custom_call" | custom-call | flops 4227858432 | tf_op jit(solution)/shard_map/pallas_call | solution.py:168
  113.2 2.9 %shard_map.76.refs_9_ = f32[3,64,128]{2,1,0:T(8,128)S(1)} custom-call(s32[2]{0:T(128)S(1)} %pad_add_fusion.pos_ref, bf16[16,32,512]{2,1,0:T(8,128)(2,1)S(1)} %turn.1.r0.refs_4_.refs_7_, bf16[16,32,512]{2,1,0:T(8,128)(2,1)S(1)} %collective-permute-done.11.r1.refs_5_.refs_8_, bf16[16,32,512]{2,1,0:T(8,128)(2,1)S(1)} %collective-permute-done.12.r2.refs_6_.refs_9_, ...), custom_call_target="tpu_custom_call" | custom-call | flops 4325376 | bytes 8388608 | tf_op jit(solution)/shard_map/pallas_call | solution.py:224
  116.1 1.2 collective-permute-start.9
  117.9 5.8 %shard_map.77.refs_12_ = f32[3,64,128]{2,1,0:T(8,128)S(1)} custom-call(s32[2]{0:T(128)S(1)} %pad_add_fusion.pos_ref, bf16[128,3584]{1,0:T(8,128)(2,1)S(1)} %collective-permute-done.14.refs_0_, bf16[128,3584]{1,0:T(8,128)(2,1)S(1)} %collective-permute-done.15.refs_1_, bf16[128,3584]{1,0:T(8,128)(2,1)S(1)} %collective-permute-done.16.refs_2_, ...), custom_call_target="tpu_custom_call" | custom-call | flops 4227858432 | tf_op jit(solution)/shard_map/pallas_call | solution.py:275
  123.7 4.5 %shard_map.78 = f32[128,1,192]{2,1,0:T(1,128)S(1)} custom-call(s32[2]{0:T(128)S(1)} %pad_add_fusion.pos_ref, bf16[48,3584]{1,0:T(8,128)(2,1)S(1)} %collective-permute-done.2.refs_0_, bf16[32,3584]{1,0:T(8,128)(2,1)S(1)} %collective-permute-done.5.refs_1_, bf16[48,3584]{1,0:T(8,128)(2,1)S(1)} %collective-permute-done.7.refs_2_, ...), custom_call_target="tpu_custom_call" | custom-call | flops 2818572288 | tf_op jit(solution)/shard_map/pallas_call | solution.py:275
  128.2 17.2 %all_to_all.10.parts_ref = f32[128,1,192]{2,1,0:T(1,128)S(1)} all-to-all(f32[128,1,192]{2,1,0:T(1,128)S(1)} %shard_map.78), channel_id=1, replica_groups=mesh['dp'=16,'group'=8] {'dp','group'}, dimensions={0} | all-to-all | bytes 196608 | tf_op jit(solution)/shard_map/all_to_all | solution.py:338
  145.4 0.8 finish.1
  (37 shorter events, 2.5 us)
Async XLA Ops:
  0.0 18.6 %copy-start.3 = (bf16[1,512,512]{2,1,0:T(8,128)(2,1)S(1)}, bf16[1,512,512]{2,1,0:T(8,128)(2,1)}, u32[]{:S(2)}) copy-start(bf16[1,512,512]{2,1,0:T(8,128)(2,1)} %basis_ref.3) | copy-start | bytes 1572868
  1.9 16.7 %all-to-all-start = ((bf16[16,32,512]{2,1,0:T(8,128)(2,1)}), bf16[16,32,512]{2,1,0:T(8,128)(2,1)S(1)}, u32[]{:S(2)}, u32[]{:S(2)}) async-start(bf16[16,32,512]{2,1,0:T(8,128)(2,1)} %cut.1), calls=%async_computation | async-start | bytes 1048576 | tf_op jit(solution)/shard_map/all_to_all | solution.py:316
  9.1 29.0 %collective-permute-start = (bf16[128,3584]{1,0:T(8,128)(2,1)}, bf16[128,3584]{1,0:T(8,128)(2,1)}, u32[]{:S(2)}, u32[]{:S(2)}) collective-permute-start(bf16[128,3584]{1,0:T(8,128)(2,1)} %refs_0_.1), channel_id=1, source_target_pairs={{0,16},{8,24},{16,32},{24,40},{32,48},{40,56},{48,0},{56,8},{64,80... | collective-permute-start | bytes 2752520 | tf_op jit(solution)/shard_map/ppermute | solution.py:302
  10.5 30.6 %collective-permute-start.3 = (bf16[128,3584]{1,0:T(8,128)(2,1)}, bf16[128,3584]{1,0:T(8,128)(2,1)}, u32[]{:S(2)}, u32[]{:S(2)}) collective-permute-start(bf16[128,3584]{1,0:T(8,128)(2,1)} %refs_0_.1), channel_id=1, source_target_pairs={{0,64},{8,72},{16,80},{24,88},{32,96},{40,104},{48,112},{56,120},{... | collective-permute-start | bytes 2752520 | tf_op jit(solution)/shard_map/ppermute | solution.py:302
  11.6 29.8 %collective-permute-start.18 = (bf16[128,3584]{1,0:T(8,128)(2,1)}, bf16[128,3584]{1,0:T(8,128)(2,1)}, u32[]{:S(2)}, u32[]{:S(2)}) collective-permute-start(bf16[128,3584]{1,0:T(8,128)(2,1)} %refs_0_.1), channel_id=1, source_target_pairs={{0,48},{8,56},{16,0},{24,8},{32,16},{40,24},{48,32},{56,40},{64,11... | collective-permute-start | bytes 2752520 | tf_op jit(solution)/shard_map/ppermute | solution.py:302
  13.1 29.5 %collective-permute-start.17 = (bf16[128,3584]{1,0:T(8,128)(2,1)}, bf16[128,3584]{1,0:T(8,128)(2,1)}, u32[]{:S(2)}, u32[]{:S(2)}) collective-permute-start(bf16[128,3584]{1,0:T(8,128)(2,1)} %refs_0_.1), channel_id=1, source_target_pairs={{0,8},{8,0},{16,24},{24,16},{32,40},{40,32},{48,56},{56,48},{64,72... | collective-permute-start | bytes 2752520 | tf_op jit(solution)/shard_map/ppermute | solution.py:302
  19.1 23.6 %collective-permute-start.11 = (bf16[16,32,512]{2,1,0:T(8,128)(2,1)S(1)}, bf16[16,32,512]{2,1,0:T(8,128)(2,1)S(1)}, u32[]{:S(2)}, u32[]{:S(2)}) collective-permute-start(bf16[16,32,512]{2,1,0:T(8,128)(2,1)S(1)} %turn.1.r0.refs_4_.refs_7_), channel_id=1, source_target_pairs={{0,3},{1,0},{2,1},{3,2},{4,7},{5,4},{6,5},{7,6},{8,11},{9,8},{10,9... | collective-permute-start | bytes 1572872 | tf_op jit(solution)/shard_map/ppermute | solution.py:302
  38.1 14.2 %collective-permute-start.12 = (bf16[16,32,512]{2,1,0:T(8,128)(2,1)S(1)}, bf16[16,32,512]{2,1,0:T(8,128)(2,1)S(1)}, u32[]{:S(2)}, u32[]{:S(2)}) collective-permute-start(bf16[16,32,512]{2,1,0:T(8,128)(2,1)S(1)} %turn.1.r0.refs_4_.refs_7_), channel_id=1, source_target_pairs={{0,2},{1,3},{2,0},{3,1},{4,6},{5,7},{6,4},{7,5},{8,10},{9,11},{10,... | collective-permute-start | bytes 1572872 | tf_op jit(solution)/shard_map/ppermute | solution.py:302
  41.0 23.8 %collective-permute-start.13 = (bf16[16,32,512]{2,1,0:T(8,128)(2,1)S(1)}, bf16[16,32,512]{2,1,0:T(8,128)(2,1)S(1)}, u32[]{:S(2)}, u32[]{:S(2)}) collective-permute-start(bf16[16,32,512]{2,1,0:T(8,128)(2,1)S(1)} %turn.1.r0.refs_4_.refs_7_), channel_id=1, source_target_pairs={{0,1},{1,2},{2,3},{3,0},{4,5},{5,6},{6,7},{7,4},{8,9},{9,10},{10,1... | collective-permute-start | bytes 1572872 | tf_op jit(solution)/shard_map/ppermute | solution.py:302
  41.4 39.4 %collective-permute-start.1 = (bf16[128,3584]{1,0:T(8,128)(2,1)}, bf16[128,3584]{1,0:T(8,128)(2,1)S(1)}, u32[]{:S(2)}, u32[]{:S(2)}) collective-permute-start(bf16[128,3584]{1,0:T(8,128)(2,1)} %collective-permute-done.refs_2_), channel_id=1, source_target_pairs={{0,64},{8,72},{16,80},{24,88},{32,96},{40,104},{48,112},{56,120},{... | collective-permute-start | bytes 2752520 | tf_op jit(solution)/shard_map/ppermute | solution.py:302
  42.6 38.3 %collective-permute-start.6 = (bf16[128,3584]{1,0:T(8,128)(2,1)}, bf16[128,3584]{1,0:T(8,128)(2,1)}, u32[]{:S(2)}, u32[]{:S(2)}) collective-permute-start(bf16[128,3584]{1,0:T(8,128)(2,1)} %collective-permute-done.refs_2_), channel_id=1, source_target_pairs={{0,16},{8,24},{16,32},{24,40},{32,48},{40,56},{48,0},{56,8},{64,80... | collective-permute-start | bytes 2752520 | tf_op jit(solution)/shard_map/ppermute | solution.py:302
  42.6 38.7 %collective-permute-start.4 = (bf16[128,3584]{1,0:T(8,128)(2,1)}, bf16[128,3584]{1,0:T(8,128)(2,1)}, u32[]{:S(2)}, u32[]{:S(2)}) collective-permute-start(bf16[128,3584]{1,0:T(8,128)(2,1)} %collective-permute-done.3.refs_4_), channel_id=1, source_target_pairs={{0,48},{8,56},{16,0},{24,8},{32,16},{40,24},{48,32},{56,40},{64,11... | collective-permute-start | bytes 2752520 | tf_op jit(solution)/shard_map/ppermute | solution.py:302
  52.4 29.1 %collective-permute-start.19 = (bf16[128,3584]{1,0:T(8,128)(2,1)}, bf16[128,3584]{1,0:T(8,128)(2,1)}, u32[]{:S(2)}, u32[]{:S(2)}) collective-permute-start(bf16[128,3584]{1,0:T(8,128)(2,1)} %collective-permute-done.refs_2_), channel_id=1, source_target_pairs={{0,8},{8,0},{16,24},{24,16},{32,40},{40,32},{48,56},{56,48},{64,72... | collective-permute-start | bytes 2752520 | tf_op jit(solution)/shard_map/ppermute | solution.py:302
  64.8 33.2 %collective-permute-start.21 = (bf16[128,3584]{1,0:T(8,128)(2,1)}, bf16[128,3584]{1,0:T(8,128)(2,1)}, u32[]{:S(2)}, u32[]{:S(2)}) collective-permute-start(bf16[128,3584]{1,0:T(8,128)(2,1)} %collective-permute-done.3.refs_4_), channel_id=1, source_target_pairs={{0,8},{8,0},{16,24},{24,16},{32,40},{40,32},{48,56},{56,48},{64,72... | collective-permute-start | bytes 2752520 | tf_op jit(solution)/shard_map/ppermute | solution.py:302
  80.8 23.9 %collective-permute-start.20 = (bf16[128,3584]{1,0:T(8,128)(2,1)}, bf16[128,3584]{1,0:T(8,128)(2,1)S(1)}, u32[]{:S(2)}, u32[]{:S(2)}) collective-permute-start(bf16[128,3584]{1,0:T(8,128)(2,1)} %collective-permute-done.18.refs_3_), channel_id=1, source_target_pairs={{0,8},{8,0},{16,24},{24,16},{32,40},{40,32},{48,56},{56,48},{64,72... | collective-permute-start | bytes 2752520 | tf_op jit(solution)/shard_map/ppermute | solution.py:302
  80.9 36.7 %collective-permute-start.14 = (bf16[128,3584]{1,0:T(8,128)(2,1)}, bf16[128,3584]{1,0:T(8,128)(2,1)S(1)}, u32[]{:S(2)}, u32[]{:S(2)}) collective-permute-start(bf16[128,3584]{1,0:T(8,128)(2,1)} %collective-permute-done.6.refs_0_), channel_id=1, source_target_pairs={{0,8},{8,0},{16,24},{24,16},{32,40},{40,32},{48,56},{56,48},{64,72... | collective-permute-start | bytes 2752520 | tf_op jit(solution)/shard_map/ppermute | solution.py:302
  81.3 36.5 %collective-permute-start.16 = (bf16[128,3584]{1,0:T(8,128)(2,1)S(1)}, bf16[128,3584]{1,0:T(8,128)(2,1)S(1)}, u32[]{:S(2)}, u32[]{:S(2)}) collective-permute-start(bf16[128,3584]{1,0:T(8,128)(2,1)S(1)} %collective-permute-done.1.refs_2_), channel_id=1, source_target_pairs={{0,8},{8,0},{16,24},{24,16},{32,40},{40,32},{48,56},{56,48},{64,72... | collective-permute-start | bytes 2752520 | tf_op jit(solution)/shard_map/ppermute | solution.py:302
  81.5 36.4 %collective-permute-start.15 = (bf16[128,3584]{1,0:T(8,128)(2,1)}, bf16[128,3584]{1,0:T(8,128)(2,1)S(1)}, u32[]{:S(2)}, u32[]{:S(2)}) collective-permute-start(bf16[128,3584]{1,0:T(8,128)(2,1)} %collective-permute-done.4.refs_1_), channel_id=1, source_target_pairs={{0,8},{8,0},{16,24},{24,16},{32,40},{40,32},{48,56},{56,48},{64,72... | collective-permute-start | bytes 2752520 | tf_op jit(solution)/shard_map/ppermute | solution.py:302
  81.8 4.1 %copy-start = (bf16[3,3584,512]{2,1,0:T(8,128)(2,1)S(1)}, bf16[3,3584,512]{2,1,0:T(8,128)(2,1)}, u32[]{:S(2)}) copy-start(bf16[3,3584,512]{2,1,0:T(8,128)(2,1)} %early.1.refs_5_.refs_3_.refs_6_) | copy-start | bytes 33030148
  86.0 12.5 %copy-start.1 = (bf16[3,3584,512]{2,1,0:T(8,128)(2,1)S(1)}, bf16[3,3584,512]{2,1,0:T(8,128)(2,1)}, u32[]{:S(2)}) copy-start(bf16[3,3584,512]{2,1,0:T(8,128)(2,1)} %early.1.refs_5_.refs_3_.refs_6_) | copy-start | bytes 33030148
  98.0 8.0 %collective-permute-start.5 = (bf16[32,3584]{1,0:T(8,128)(2,1)S(1)}, bf16[32,3584]{1,0:T(8,128)(2,1)S(1)}, u32[]{:S(2)}, u32[]{:S(2)}) collective-permute-start(bf16[32,3584]{1,0:T(8,128)(2,1)S(1)} %slice.13), channel_id=1, source_target_pairs={{0,48},{8,56},{16,0},{24,8},{32,16},{40,24},{48,32},{56,40},{64,11... | collective-permute-start | bytes 688136 | tf_op jit(solution)/shard_map/ppermute | solution.py:302
  104.7 8.6 %copy-start.2 = (s32[2048]{0:T(1024)S(1)}, s32[2048]{0:T(1024)}, u32[]{:S(2)}) copy-start(s32[2048]{0:T(1024)} %param.13) | copy-start | bytes 24580
  104.7 11.4 %collective-permute-start.7 = (bf16[48,3584]{1,0:T(8,128)(2,1)S(1)}, bf16[48,3584]{1,0:T(8,128)(2,1)S(1)}, u32[]{:S(2)}, u32[]{:S(2)}) collective-permute-start(bf16[48,3584]{1,0:T(8,128)(2,1)S(1)} %slice.14), channel_id=1, source_target_pairs={{0,64},{8,72},{16,80},{24,88},{32,96},{40,104},{48,112},{56,120},{... | collective-permute-start | bytes 1032200 | tf_op jit(solution)/shard_map/ppermute | solution.py:302
  106.0 11.4 %collective-permute-start.2 = (bf16[48,3584]{1,0:T(8,128)(2,1)S(1)}, bf16[48,3584]{1,0:T(8,128)(2,1)S(1)}, u32[]{:S(2)}, u32[]{:S(2)}) collective-permute-start(bf16[48,3584]{1,0:T(8,128)(2,1)S(1)} %slice.12), channel_id=1, source_target_pairs={{0,16},{8,24},{16,32},{24,40},{32,48},{40,56},{48,0},{56,8},{64,80... | collective-permute-start | bytes 1032200 | tf_op jit(solution)/shard_map/ppermute | solution.py:302
  116.1 7.6 %collective-permute-start.9 = (bf16[32,3584]{1,0:T(8,128)(2,1)S(1)}, bf16[32,3584]{1,0:T(8,128)(2,1)S(1)}, u32[]{:S(2)}, u32[]{:S(2)}) collective-permute-start(bf16[32,3584]{1,0:T(8,128)(2,1)S(1)} %collective-permute-done.5.refs_1_), channel_id=1, source_target_pairs={{0,8},{8,0},{16,24},{24,16},{32,40},{40,32},{48,56},{56,48},{64,72... | collective-permute-start | bytes 688136 | tf_op jit(solution)/shard_map/ppermute | solution.py:302
  117.3 6.4 %collective-permute-start.10 = (bf16[48,3584]{1,0:T(8,128)(2,1)S(1)}, bf16[48,3584]{1,0:T(8,128)(2,1)S(1)}, u32[]{:S(2)}, u32[]{:S(2)}) collective-permute-start(bf16[48,3584]{1,0:T(8,128)(2,1)S(1)} %collective-permute-done.7.refs_2_), channel_id=1, source_target_pairs={{0,8},{8,0},{16,24},{24,16},{32,40},{40,32},{48,56},{56,48},{64,72... | collective-permute-start | bytes 1032200 | tf_op jit(solution)/shard_map/ppermute | solution.py:302
  117.7 6.1 %collective-permute-start.8 = (bf16[48,3584]{1,0:T(8,128)(2,1)S(1)}, bf16[48,3584]{1,0:T(8,128)(2,1)S(1)}, u32[]{:S(2)}, u32[]{:S(2)}) collective-permute-start(bf16[48,3584]{1,0:T(8,128)(2,1)S(1)} %collective-permute-done.2.refs_0_), channel_id=1, source_target_pairs={{0,8},{8,0},{16,24},{24,16},{32,40},{40,32},{48,56},{56,48},{64,72... | collective-permute-start | bytes 1032200 | tf_op jit(solution)/shard_map/ppermute | solution.py:302

commit v2 on v1

--- a/solution.py
+++ b/solution.py
@@ -98,7 +98,7 @@
             out_specs=pl.BlockSpec((16, quarter, BLK), lambda i, d: (0, 0, 0)),
             scratch_shapes=[pltpu.VMEM((16 * quarter, BLK), BF16)],
         ),
-        cost_estimate=pl.CostEstimate(flops=10**10, bytes_accessed=3 << 19, transcendentals=0),
+        cost_estimate=pl.CostEstimate(flops=4 * 10**10, bytes_accessed=3 << 19, transcendentals=0),
         compiler_params=pltpu.CompilerParams(vmem_limit_bytes=8 << 20),
         name="turn",
     )(dp, rows, basis)
@@ -149,32 +149,42 @@
 resident = lambda v: pltpu.with_memory_space_constraint(v, pltpu.VMEM)
 
 
-def product_kernel(*refs):
-    row_refs, (weight_ref, out_ref) = refs[:-2], refs[-2:]
-
-    def body(q, carry):
+def product_kernel(count, *refs):
+    row_refs, weight_ref, far_refs = refs[:count], refs[count], refs[count + 1:]
+    moved = (len(far_refs) - 1) // 2
+    if moved:
+        far_refs, out_ref, near_refs, sems = far_refs[:moved], far_refs[moved], far_refs[moved + 1:-1], far_refs[-1]
+        copies = [
+            pltpu.make_async_copy(far, near, sems.at[i]) for i, (far, near) in enumerate(zip(far_refs, near_refs))
+        ]
+    else:
+        out_ref, copies = far_refs[0], []
+    for copy in copies:
+        copy.start()
+    for q in range(Q):
         for part in range(BLK // TILE):
+            columns = slice(part * TILE, (part + 1) * TILE)
             rows = jnp.concatenate([ref[...] for ref in row_refs], axis=0)
-            tile = weight_ref[q, :, part * TILE:(part + 1) * TILE]
-            out_ref[q, :, part * TILE:(part + 1) * TILE] = jnp.dot(rows, tile, preferred_element_type=F32)
-        return carry
-
-    lax.fori_loop(0, Q, body, 0)
-
-
-def product(rows, weight):
+            out_ref[q, :, columns] = jnp.dot(rows, weight_ref[q, :, columns], preferred_element_type=F32)
+    for copy in copies:
+        copy.wait()
+
+
+def product(rows, weight, far=()):
     height = sum(r.shape[0] for r in rows)
     depth = weight.shape[1]
-    return pl.pallas_call(
-        product_kernel,
-        out_shape=pltpu.VMEM((Q, height, BLK), F32),
-        in_specs=[WHOLE] * (len(rows) + 1),
-        out_specs=WHOLE,
+    outs = pl.pallas_call(
+        functools.partial(product_kernel, len(rows)),
+        out_shape=(pltpu.VMEM((Q, height, BLK), F32),) + tuple(pltpu.VMEM(v.shape, v.dtype) for v in far),
+        in_specs=[WHOLE] * (len(rows) + 1) + [pl.BlockSpec(memory_space=pltpu.HBM)] * len(far),
+        out_specs=(WHOLE,) * (1 + len(far)),
+        scratch_shapes=[pltpu.SemaphoreType.DMA((len(far),))] if far else [],
         cost_estimate=pl.CostEstimate(
             flops=2 * height * depth * Q * BLK, bytes_accessed=0, transcendentals=0
         ),
         compiler_params=pltpu.CompilerParams(vmem_limit_bytes=8 << 20),
-    )(*[resident(r) for r in rows], resident(weight))
+    )(*[resident(r) for r in rows], resident(weight), *[distant(v) for v in far])
+    return outs if far else outs[0]
 
 
 def place(inputs, pieces, y, first):
@@ -189,95 +199,97 @@
     return sum([values[:, i:i + 128] for i in range(128, values.shape[1], 128)], values[:, :128])
 
 
-def doc_sums(dp, offsets, ids_ref, tokens, before):
+def doc_sums(dp, offsets, ids_ref, tokens):
     docs = lax.broadcasted_iota(jnp.int32, (DOCS, ROWS), 0)
     member = jnp.concatenate(
         [(docs == ids_ref[source(dp, offset)]).astype(F32) for offset in offsets], axis=1
-    )
-    return [
-        before[q] + jnp.dot(member, tokens[q], precision=HIGHEST, preferred_element_type=F32) for q in range(Q)
-    ]
-
-
-def settle_kernel(offsets, first, counts, pos_ref, r0, r1, r2, r3, ids_ref, *refs):
+    ).astype(BF16)
+    total = jnp.zeros((DOCS, Q * 128), F32)
+    for _ in range(3):
+        term = tokens.astype(BF16)
+        total = total + jnp.dot(member, term, preferred_element_type=F32)
+        tokens = tokens - term.astype(F32)
+    return total
+
+
+STRIP = 64
+
+
+def settle_kernel(offsets, first, pos_ref, r0, r1, r2, r3, ids_ref, *refs):
     projected, (out_ref, inputs, tokens) = refs[:-3], refs[-3:]
     dp, y = pos_ref[0], pos_ref[1]
     place(inputs, (r0, r1, r2, r3), y, first)
-
-    def body(q, carry):
-        start = 0
-        for ref, count in zip(projected, counts):
-            for k in range(count):
-                values = ref[q, k * ROWS:(k + 1) * ROWS, :] * inputs[start:start + ROWS, :].astype(F32)
-                tokens[q, start:start + ROWS] = narrowed(values)
-                start += ROWS
-        return carry
-
-    lax.fori_loop(0, Q, body, 0)
-    for q, sums in enumerate(doc_sums(dp, offsets, ids_ref, tokens, (0.0,) * Q)):
-        out_ref[q] = sums
+    base = 0
+    for ref in projected:
+
+        def body(i, carry, ref=ref, base=base):
+            here = pl.multiple_of(i * STRIP, STRIP)
+            there = pl.ds(pl.multiple_of(base + here, STRIP), STRIP)
+            wide = inputs[there, :].astype(F32)
+            for q in range(Q):
+                values = ref[q, pl.ds(here, STRIP), :] * wide
+                tokens[there, q * 128:(q + 1) * 128] = narrowed(values)
+            return carry
+
+        lax.fori_loop(0, ref.shape[1] // STRIP, body, 0)
+        base += ref.shape[1]
+    out_ref[...] = doc_sums(dp, offsets, ids_ref, tokens[...])
 
 
 def settle(position, projected, offsets, first, pieces, ids):
-    counts = tuple(p.shape[1] // ROWS for p in projected)
     height = len(offsets) * ROWS
     return pl.pallas_call(
-        functools.partial(settle_kernel, offsets, first, counts),
-        out_shape=jax.ShapeDtypeStruct((Q, DOCS, 128), F32),
+        functools.partial(settle_kernel, offsets, first),
+        out_shape=jax.ShapeDtypeStruct((DOCS, Q * 128), F32),
         in_specs=[SCALARS] + [WHOLE] * (5 + len(projected)),
         out_specs=WHOLE,
-        scratch_shapes=[pltpu.VMEM((height, BLK), BF16), pltpu.VMEM((Q, height, 128), F32)],
+        scratch_shapes=[pltpu.VMEM((height, BLK), BF16), pltpu.VMEM((height, Q * 128), F32)],
         cost_estimate=pl.CostEstimate(
             flops=2 * height * Q * BLK, bytes_accessed=8 << 20, transcendentals=0
         ),
-        compiler_params=pltpu.CompilerParams(vmem_limit_bytes=8 << 20),
+        compiler_params=pltpu.CompilerParams(vmem_limit_bytes=12 << 20),
     )(position, *[resident(p) for p in pieces], resident(ids), *[resident(p) for p in projected])
 
 
-def score_kernel(offsets, first, last, pos_ref, *refs):
-    row_refs, refs = refs[:-10], refs[-10:]
-    weight_ref, r0, r1, r2, r3, ids_ref, before_ref, out_ref, inputs, tokens = refs
+def score_kernel(offsets, first, pos_ref, *refs):
+    row_refs, refs = refs[:-11], refs[-11:]
+    weight_ref, r0, r1, r2, r3, ids_ref, before_ref, done_ref, out_ref, inputs, tokens = refs
     dp, y = pos_ref[0], pos_ref[1]
     place(inputs, (r0, r1, r2, r3), y, first)
-
-    def body(q, carry):
+    done = done_ref.shape[1]
+    for q in range(Q):
         for part in range(BLK // TILE):
             columns = slice(part * TILE, (part + 1) * TILE)
             rows = jnp.concatenate([ref[...] for ref in row_refs], axis=0)
             values = jnp.dot(rows, weight_ref[q, :, columns], preferred_element_type=F32)
-            narrow = narrowed(values * inputs[:, columns].astype(F32))
+            narrow = narrowed(values * inputs[done:, columns].astype(F32))
+            lanes = slice(q * 128, (q + 1) * 128)
             if part == 0:
-                tokens[q] = narrow
+                tokens[done:, lanes] = narrow
             else:
-                tokens[q] += narrow
-        return carry
-
-    lax.fori_loop(0, Q, body, 0)
-    sums = doc_sums(dp, offsets, ids_ref, tokens, [before_ref[q] for q in range(Q)])
-    if last:
-        flat = lax.dot_general(
-            jnp.ones((8, 128), F32),
-            jnp.concatenate(sums, axis=0),
-            (((1,), (1,)), ((), ())),
-            precision=HIGHEST,
-            preferred_element_type=F32,
-        )
-        out_ref[...] = jnp.broadcast_to(flat[None, :1], out_ref.shape)
-    else:
-        for q in range(Q):
-            out_ref[q] = sums[q]
-
-
-def score(position, rows, offsets, first, weight, pieces, ids, before, last=False):
+                tokens[done:, lanes] += narrow
+    for q in range(Q):
+        tokens[:done, q * 128:(q + 1) * 128] = narrowed(done_ref[q] * inputs[:done, :].astype(F32))
+    sums = before_ref[...] + doc_sums(dp, offsets, ids_ref, tokens[...])
+    flat = lax.dot_general(
+        jnp.ones((8, 128), F32),
+        jnp.concatenate([sums[:, q * 128:(q + 1) * 128] for q in range(Q)], axis=0),
+        (((1,), (1,)), ((), ())),
+        precision=HIGHEST,
+        preferred_element_type=F32,
+    )
+    out_ref[...] = jnp.broadcast_to(flat[None, :1], out_ref.shape)
+
+
+def score(position, rows, offsets, first, weight, pieces, ids, before, done):
     height = len(offsets) * ROWS
     depth = weight.shape[1]
-    out = (128, 1, Q * DOCS) if last else (Q, DOCS, 128)
-    return pl.pallas_call(
-        functools.partial(score_kernel, offsets, first, last),
-        out_shape=jax.ShapeDtypeStruct(out, F32),
-        in_specs=[SCALARS] + [WHOLE] * (len(rows) + 7),
+    return pl.pallas_call(
+        functools.partial(score_kernel, offsets, first),
+        out_shape=jax.ShapeDtypeStruct((128, 1, Q * DOCS), F32),
+        in_specs=[SCALARS] + [WHOLE] * (len(rows) + 8),
         out_specs=WHOLE,
-        scratch_shapes=[pltpu.VMEM((height, BLK), BF16), pltpu.VMEM((Q, height, 128), F32)],
+        scratch_shapes=[pltpu.VMEM((height, BLK), BF16), pltpu.VMEM((height, Q * 128), F32)],
         cost_estimate=pl.CostEstimate(
             flops=2 * height * depth * Q * BLK, bytes_accessed=0, transcendentals=0
         ),
@@ -289,6 +301,7 @@
         *[resident(p) for p in pieces],
         resident(ids),
         resident(before),
+        resident(done),
     )
 
 
@@ -325,15 +338,20 @@
     b3 = move(a3, ACROSS)
     b1 = move(b0, LEFT)
     step1 = [move(v, MATE) for v in (a3, a1, b0)]
-    parts = [move(b3[:48], RIGHT), move(b1[48:80], LEFT), move(a2[80:], ACROSS)]
+    parts = [move(b3[:64], RIGHT), move(b1[64:], LEFT)]
     step2 = [move(v, MATE) for v in (a2, b1, b3)]
     step3 = [move(v, MATE) for v in parts]
 
-    projected = [product([out_grads, mate, a3, a1, b0], weight), product(step1, weight)]
-    projected.append(product([a2, b1, b3], weight))
-    total = settle(position, projected, ORDER[:11], 0, pieces, ids)
-    total = score(position, step2, ORDER[11:14], 11, weight, pieces, ids, total)
-    partial = score(position, parts + step3, ORDER[14:], 14, weight, pieces, ids, total, True)
+    second, *near = product(step1, weight, (a3, a1, b0))
+    projected = [
+        product([out_grads, mate] + near, weight),
+        second,
+        product([a2, b1, b3], weight),
+        product(step2, weight),
+    ]
+    total = settle(position, projected, ORDER[:14], 0, pieces, ids)
+    done = product(parts, weight)
+    partial = score(position, step3, ORDER[14:], 14, weight, pieces, ids, total, done)
 
     partials = lax.all_to_all(partial, ("dp", "group"), 0, 0, tiled=True)
     return pl.pallas_call(

time: 147 us -> 140 us (0.952)
  waiting for transfers between devices: 37.1 us -> 43.2 us
  Pallas kernels: 54.3 us -> 48.8 us
  local copies, waits for them, and re-layouts: 6.12 us -> 2.03 us
  starting transfers between devices: 31.3 us -> 27.6 us
    ppermute x22 -> x20, waiting for transfers between devices: 32.9 us -> 42.6 us  [move(): return lax.ppermute(v, axis, perm)]
    pallas_call x6 -> x7, Pallas kernels: 35.6 us -> 30.2 us  [the longest x5 25 us: product(): pl.pallas_call(functools.partial(product_kernel, len(rows)), out_shape=(p...]
    all_to_all x1, starting transfers between devices: 7.16 us -> 3.47 us  [on_device(): lax.all_to_all(cut(activations, position[1:]), 'dp', 0, 0, tiled=True)]
    all_to_all x1, waiting for transfers between devices: 4.23 us -> 0.59 us  [on_device(): lax.all_to_all(cut(activations, position[1:]), 'dp', 0, 0, tiled=True)]
    unnamed x8 -> x10, local copies, waits for them, and re-layouts: 4.14 us -> 1.96 us
    slice x3 -> x2, local copies, waits for them, and re-layouts: 1.98 us -> 0.06 us  [on_device(): parts = [move(b3[:64], RIGHT), move(b1[64:], LEFT)]]
    ppermute x22 -> x20, starting transfers between devices: 24.1 us -> 24.1 us  [move(): return lax.ppermute(v, axis, perm)]
  transfers between devices with their start and end apart: 23 -> 21, of which waited for: 4 -> 5; matrix products, arithmetic and copies ran while one was open for 1% -> 0% of each run, Pallas kernels for 32% -> 33%
where the time goes in v2:
time: 140 us; the launch traced here: 139 us
  Pallas kernels  48.8 us (35%)
  waiting for transfers between devices  43.2 us (31%)
  starting transfers between devices  27.6 us (20%)
  blocking collectives  17.3 us (12%)
  local copies, waits for them, and re-layouts  2.03 us (1%)
    ppermute x20, waiting for transfers between devices, move(): return lax.ppermute(v, axis, perm)  42.6 us
    pallas_call x5, Pallas kernels, product(): pl.pallas_call(functools.partial(product_kernel, len(rows)), out_shape=(p...  25 us
    ppermute x20, starting transfers between devices, move(): return lax.ppermute(v, axis, perm)  24.1 us
    all_to_all x1, blocking collectives, on_device(): partials = lax.all_to_all(partial, ('dp', 'group'), 0, 0, tiled=True)  17.3 us
    pallas_call x1, Pallas kernels, fold_early(): pl.pallas_call(early_kernel, out_shape=jax.ShapeDtypeStruct((Q, nblocks *...  15.5 us
    all_to_all x1, starting transfers between devices, on_device(): lax.all_to_all(cut(activations, position[1:]), 'dp', 0, 0, tiled=True)  3.47 us
  transfers between devices with their start and end apart: 21, of which 5 were waited for; matrix products, arithmetic and copies ran while one was open for 0% of the time, Pallas kernels for 33%

profile of v2, /device:TPU:1, one launch (start us, length us, event | category | flops | bytes accessed | tf_op | source)
XLA Modules:
  0.0 139.2 jit_solution(7205985179088759973)
XLA Ops:
  0.0 2.0 %collective-permute-start = (bf16[128,3584]{1,0:T(8,128)(2,1)}, bf16[128,3584]{1,0:T(8,128)(2,1)}, u32[]{:S(2)}, u32[]{:S(2)}) collective-permute-start(bf16[128,3584]{1,0:T(8,128)(2,1)} %refs_0_.1), channel_id=1, source_target_pairs={{0,16},{8,24},{16,32},{24,40},{32,48},{40,56},{48,0},{56,8},{64,80... | collective-permute-start | bytes 2752520 | tf_op jit(solution)/shard_map/ppermute | solution.py:315
  2.0 1.6 %collective-permute-start.4 = (bf16[128,3584]{1,0:T(8,128)(2,1)}, bf16[128,3584]{1,0:T(8,128)(2,1)}, u32[]{:S(2)}, u32[]{:S(2)}) collective-permute-start(bf16[128,3584]{1,0:T(8,128)(2,1)} %refs_0_.1), channel_id=1, source_target_pairs={{0,64},{8,72},{16,80},{24,88},{32,96},{40,104},{48,112},{56,120},{... | collective-permute-start | bytes 2752520 | tf_op jit(solution)/shard_map/ppermute | solution.py:315
  3.7 1.5 %collective-permute-start.13 = (bf16[128,3584]{1,0:T(8,128)(2,1)}, bf16[128,3584]{1,0:T(8,128)(2,1)S(1)}, u32[]{:S(2)}, u32[]{:S(2)}) collective-permute-start(bf16[128,3584]{1,0:T(8,128)(2,1)} %refs_0_.1), channel_id=1, source_target_pairs={{0,48},{8,56},{16,0},{24,8},{32,16},{40,24},{48,32},{56,40},{64,11... | collective-permute-start | bytes 2752520 | tf_op jit(solution)/shard_map/ppermute | solution.py:315
  5.1 18.2 %collective-permute-done.refs_4_ = bf16[128,3584]{1,0:T(8,128)(2,1)} collective-permute-done((bf16[128,3584]{1,0:T(8,128)(2,1)}, bf16[128,3584]{1,0:T(8,128)(2,1)}, u32[]{:S(2)}, u32[]{:S(2)}) %collective-permute-start) | collective-permute-done | bytes 917536 | tf_op jit(solution)/shard_map/ppermute | solution.py:315
  23.3 1.9 %collective-permute-start.1 = (bf16[128,3584]{1,0:T(8,128)(2,1)}, bf16[128,3584]{1,0:T(8,128)(2,1)S(1)}, u32[]{:S(2)}, u32[]{:S(2)}) collective-permute-start(bf16[128,3584]{1,0:T(8,128)(2,1)} %collective-permute-done.refs_4_), channel_id=1, source_target_pairs={{0,64},{8,72},{16,80},{24,88},{32,96},{40,104},{48,112},{56,120},{... | collective-permute-start | bytes 2752520 | tf_op jit(solution)/shard_map/ppermute | solution.py:315
  25.2 1.3 collective-permute-start.5
  26.5 2.1 %collective-permute-start.11 = (bf16[128,3584]{1,0:T(8,128)(2,1)}, bf16[128,3584]{1,0:T(8,128)(2,1)}, u32[]{:S(2)}, u32[]{:S(2)}) collective-permute-start(bf16[128,3584]{1,0:T(8,128)(2,1)} %refs_0_.1), channel_id=1, source_target_pairs={{0,8},{8,0},{16,24},{24,16},{32,40},{40,32},{48,56},{56,48},{64,72... | collective-permute-start | bytes 2752520 | tf_op jit(solution)/shard_map/ppermute | solution.py:315
  28.6 1.9 %cut.1 = bf16[16,32,512]{2,1,0:T(8,128)(2,1)} custom-call(s32[1]{0:T(128)} %bitcast.1.y_ref, bf16[128,8192]{1,0:T(8,128)(2,1)} %rows_ref.1), custom_call_target="tpu_custom_call" | custom-call | bytes 1048576 | tf_op jit(solution)/shard_map/cut/pallas_call | solution.py:63
  30.5 3.5 %all-to-all-start = ((bf16[16,32,512]{2,1,0:T(8,128)(2,1)}), bf16[16,32,512]{2,1,0:T(8,128)(2,1)S(1)}, u32[]{:S(2)}, u32[]{:S(2)}) async-start(bf16[16,32,512]{2,1,0:T(8,128)(2,1)} %cut.1), calls=%async_computation | async-start | bytes 1048576 | tf_op jit(solution)/shard_map/all_to_all | solution.py:329
  34.0 15.5 %early.1.refs_3_.refs_5_.refs_2_ = bf16[3,3584,512]{2,1,0:T(8,128)(2,1)} custom-call(bf16[7,512,512]{2,1,0:T(8,128)(2,1)} %basis_ref.2, bf16[3,3584,512]{2,1,0:T(8,128)(2,1)} %bitcast.6, bf16[3584,512]{1,0:T(8,128)(2,1)} %eigen_ref.1), custom_call_target="tpu_custom_call" | custom-call | flops 5637144576 | bytes 29360128 | tf_op jit(solution)/shard_map/early/pallas_call | solution.py:134
  50.6 1.5 %collective-permute-start.16 = (bf16[128,3584]{1,0:T(8,128)(2,1)}, bf16[128,3584]{1,0:T(8,128)(2,1)S(1)}, u32[]{:S(2)}, u32[]{:S(2)}) collective-permute-start(bf16[128,3584]{1,0:T(8,128)(2,1)} %collective-permute-done.refs_4_), channel_id=1, source_target_pairs={{0,16},{8,24},{16,32},{24,40},{32,48},{40,56},{48,0},{56,8},{64,80... | collective-permute-start | bytes 2752520 | tf_op jit(solution)/shard_map/ppermute | solution.py:315
  52.5 0.6 all-to-all-done.rows_ref
  53.1 1.0 copy-done.3
  54.7 0.7 collective-permute-start.2
  55.4 2.1 %collective-permute-start.6 = (bf16[64,3584]{1,0:T(8,128)(2,1)S(1)}, bf16[64,3584]{1,0:T(8,128)(2,1)S(1)}, u32[]{:S(2)}, u32[]{:S(2)}) collective-permute-start(bf16[64,3584]{1,0:T(8,128)(2,1)S(1)} %slice.9), channel_id=1, source_target_pairs={{0,48},{8,56},{16,0},{24,8},{32,16},{40,24},{48,32},{56,40},{64,11... | collective-permute-start | bytes 1376264 | tf_op jit(solution)/shard_map/ppermute | solution.py:315
  58.3 6.2 %shard_map.73 = (f32[3,384,512]{2,1,0:T(8,128)S(1)}, bf16[128,3584]{1,0:T(8,128)(2,1)S(1)}, bf16[128,3584]{1,0:T(8,128)(2,1)S(1)}, bf16[128,3584]{1,0:T(8,128)(2,1)S(1)}) custom-call(bf16[128,3584]{1,0:T(8,128)(2,1)} %collective-permute-done.12.refs_0_, bf16[128,3584]{1,0:T(8,128)(2,1)} %collective-permute-done.14.refs_1_, ...), custom_call_target="tpu_custom_call" | custom-call | flops 4227858432 | tf_op jit(solution)/shard_map/pallas_call | solution.py:176
  64.6 8.9 %collective-permute-done.16.refs_0_ = bf16[128,3584]{1,0:T(8,128)(2,1)S(1)} collective-permute-done((bf16[128,3584]{1,0:T(8,128)(2,1)}, bf16[128,3584]{1,0:T(8,128)(2,1)S(1)}, u32[]{:S(2)}, u32[]{:S(2)}) %collective-permute-start.16) | collective-permute-done | bytes 917536 | tf_op jit(solution)/shard_map/ppermute | solution.py:315
  73.4 2.5 %collective-permute-start.17 = (bf16[128,3584]{1,0:T(8,128)(2,1)S(1)}, bf16[128,3584]{1,0:T(8,128)(2,1)S(1)}, u32[]{:S(2)}, u32[]{:S(2)}) collective-permute-start(bf16[128,3584]{1,0:T(8,128)(2,1)S(1)} %collective-permute-done.16.refs_0_), channel_id=1, source_target_pairs={{0,8},{8,0},{16,24},{24,16},{32,40},{40,32},{48,56},{56,48},{64,72... | collective-permute-start | bytes 2752520 | tf_op jit(solution)/shard_map/ppermute | solution.py:315
  75.9 8.4 %shard_map.74.refs_0_ = f32[3,640,512]{2,1,0:T(8,128)S(1)} custom-call(bf16[128,3584]{1,0:T(8,128)(2,1)S(1)} %copy-done.2, bf16[128,3584]{1,0:T(8,128)(2,1)} %collective-permute-done.11.refs_1_, bf16[128,3584]{1,0:T(8,128)(2,1)S(1)} %get-tuple-element.9.refs_2_, bf16[128,3584]{1,0:T(8,128)(2,1)S(1)} %get-tuple-element.10.refs_3_, ...), custom_call_target="tpu_custom_call" | custom-call | flops 7046430720 | tf_op jit(solution)/shard_map/pallas_call | solution.py:176
  84.4 4.4 %shard_map.75.refs_2_ = f32[3,384,512]{2,1,0:T(8,128)S(1)} custom-call(bf16[128,3584]{1,0:T(8,128)(2,1)S(1)} %collective-permute-done.16.refs_0_, bf16[128,3584]{1,0:T(8,128)(2,1)S(1)} %collective-permute-done.5.refs_1_, bf16[128,3584]{1,0:T(8,128)(2,1)S(1)} %collective-permute-done.1.refs_2_, bf16[3,3584,512]{2,1,0:T(8,128)(2,1)S(1)} %copy-done), custom_call_target="tpu_custom_call" | custom-call | flops 4227858432 | tf_op jit(solution)/shard_map/pallas_call | solution.py:176
  88.8 1.3 collective-permute-start.10
  90.1 1.5 %collective-permute-start.8 = (bf16[16,32,512]{2,1,0:T(8,128)(2,1)S(1)}, bf16[16,32,512]{2,1,0:T(8,128)(2,1)S(1)}, u32[]{:S(2)}, u32[]{:S(2)}) collective-permute-start(bf16[16,32,512]{2,1,0:T(8,128)(2,1)S(1)} %turn.1.r0.refs_3_), channel_id=1, source_target_pairs={{0,3},{1,0},{2,1},{3,2},{4,7},{5,4},{6,5},{7,6},{8,11},{9,8},{10,9... | collective-permute-start | bytes 1572872 | tf_op jit(solution)/shard_map/ppermute | solution.py:315
  91.6 1.6 %collective-permute-start.9 = (bf16[16,32,512]{2,1,0:T(8,128)(2,1)S(1)}, bf16[16,32,512]{2,1,0:T(8,128)(2,1)S(1)}, u32[]{:S(2)}, u32[]{:S(2)}) collective-permute-start(bf16[16,32,512]{2,1,0:T(8,128)(2,1)S(1)} %turn.1.r0.refs_3_), channel_id=1, source_target_pairs={{0,2},{1,3},{2,0},{3,1},{4,6},{5,7},{6,4},{7,5},{8,10},{9,11},{10,... | collective-permute-start | bytes 1572872 | tf_op jit(solution)/shard_map/ppermute | solution.py:315
  93.2 0.8 collective-permute-start.3
  94.3 1.6 %shard_map.78.refs_9_ = f32[3,128,512]{2,1,0:T(8,128)S(1)} custom-call(bf16[64,3584]{1,0:T(8,128)(2,1)S(1)} %collective-permute-done.2.refs_0_, bf16[64,3584]{1,0:T(8,128)(2,1)S(1)} %collective-permute-done.6.refs_1_, bf16[3,3584,512]{2,1,0:T(8,128)(2,1)S(1)} %copy-done), custom_call_target="tpu_custom_call" | custom-call | flops 1409286144 | tf_op jit(solution)/shard_map/pallas_call | solution.py:176
  95.9 4.4 %shard_map.76.refs_3_ = f32[3,384,512]{2,1,0:T(8,128)S(1)} custom-call(bf16[128,3584]{1,0:T(8,128)(2,1)S(1)} %collective-permute-done.17.refs_0_, bf16[128,3584]{1,0:T(8,128)(2,1)S(1)} %collective-permute-done.18.refs_1_, bf16[128,3584]{1,0:T(8,128)(2,1)S(1)} %collective-permute-done.19.refs_2_, bf16[3,3584,512]{2,1,0:T(8,128)(2,1)S(1)} %copy-done), custom_call_target="tpu_custom_call" | custom-call | flops 4227858432 | tf_op jit(solution)/shard_map/pallas_call | solution.py:176
  100.3 3.2 %collective-permute-done.10.r3.refs_6_ = bf16[16,32,512]{2,1,0:T(8,128)(2,1)S(1)} collective-permute-done((bf16[16,32,512]{2,1,0:T(8,128)(2,1)S(1)}, bf16[16,32,512]{2,1,0:T(8,128)(2,1)S(1)}, u32[]{:S(2)}, u32[]{:S(2)}) %collective-permute-start.10) | collective-permute-done | bytes 524320 | tf_op jit(solution)/shard_map/ppermute | solution.py:315
  103.6 12.4 %collective-permute-done.9.r2.refs_5_ = bf16[16,32,512]{2,1,0:T(8,128)(2,1)S(1)} collective-permute-done((bf16[16,32,512]{2,1,0:T(8,128)(2,1)S(1)}, bf16[16,32,512]{2,1,0:T(8,128)(2,1)S(1)}, u32[]{:S(2)}, u32[]{:S(2)}) %collective-permute-start.9) | collective-permute-done | bytes 524320 | tf_op jit(solution)/shard_map/ppermute | solution.py:315
  115.9 2.5 %shard_map.77.refs_8_ = f32[64,384]{1,0:T(8,128)S(1)} custom-call(s32[2]{0:T(128)S(1)} %pad_add_fusion.pos_ref, bf16[16,32,512]{2,1,0:T(8,128)(2,1)S(1)} %turn.1.r0.refs_3_, bf16[16,32,512]{2,1,0:T(8,128)(2,1)S(1)} %collective-permute-done.8.r1.refs_4_, bf16[16,32,512]{2,1,0:T(8,128)(2,1)S(1)} %collective-permute-done.9.r2.refs_5_, ...), custom_call_target="tpu_custom_call" | custom-call | flops 5505024 | bytes 8388608 | tf_op jit(solution)/shard_map/pallas_call | solution.py:241
  118.5 2.7 %shard_map.79 = f32[128,1,192]{2,1,0:T(1,128)S(1)} custom-call(s32[2]{0:T(128)S(1)} %pad_add_fusion.pos_ref, bf16[64,3584]{1,0:T(8,128)(2,1)S(1)} %collective-permute-done.3.refs_0_, bf16[64,3584]{1,0:T(8,128)(2,1)S(1)} %collective-permute-done.7.refs_1_, bf16[3,3584,512]{2,1,0:T(8,128)(2,1)S(1)} %copy-done, bf16[16,32,512]{2,1,0:T(8,128)(2,1)S(1)} %turn.1.r0.refs_3_, ...), custom_call_target="tpu_custom_call" | custom-call | flops 2818572288 | tf_op jit(solution)/shard_map/pallas_call | solution.py:287
  121.2 17.3 %all_to_all.10.parts_ref = f32[128,1,192]{2,1,0:T(1,128)S(1)} all-to-all(f32[128,1,192]{2,1,0:T(1,128)S(1)} %shard_map.79), channel_id=1, replica_groups=mesh['dp'=16,'group'=8] {'dp','group'}, dimensions={0} | all-to-all | bytes 196608 | tf_op jit(solution)/shard_map/all_to_all | solution.py:356
  138.4 0.8 finish.1
  (35 shorter events, 3.3 us)
Async XLA Ops:
  0.0 23.3 %collective-permute-start = (bf16[128,3584]{1,0:T(8,128)(2,1)}, bf16[128,3584]{1,0:T(8,128)(2,1)}, u32[]{:S(2)}, u32[]{:S(2)}) collective-permute-start(bf16[128,3584]{1,0:T(8,128)(2,1)} %refs_0_.1), channel_id=1, source_target_pairs={{0,16},{8,24},{16,32},{24,40},{32,48},{40,56},{48,0},{56,8},{64,80... | collective-permute-start | bytes 2752520 | tf_op jit(solution)/shard_map/ppermute | solution.py:315
  2.0 23.2 %collective-permute-start.4 = (bf16[128,3584]{1,0:T(8,128)(2,1)}, bf16[128,3584]{1,0:T(8,128)(2,1)}, u32[]{:S(2)}, u32[]{:S(2)}) collective-permute-start(bf16[128,3584]{1,0:T(8,128)(2,1)} %refs_0_.1), channel_id=1, source_target_pairs={{0,64},{8,72},{16,80},{24,88},{32,96},{40,104},{48,112},{56,120},{... | collective-permute-start | bytes 2752520 | tf_op jit(solution)/shard_map/ppermute | solution.py:315
  3.7 46.0 %collective-permute-start.13 = (bf16[128,3584]{1,0:T(8,128)(2,1)}, bf16[128,3584]{1,0:T(8,128)(2,1)S(1)}, u32[]{:S(2)}, u32[]{:S(2)}) collective-permute-start(bf16[128,3584]{1,0:T(8,128)(2,1)} %refs_0_.1), channel_id=1, source_target_pairs={{0,48},{8,56},{16,0},{24,8},{32,16},{40,24},{48,32},{56,40},{64,11... | collective-permute-start | bytes 2752520 | tf_op jit(solution)/shard_map/ppermute | solution.py:315
  23.3 27.3 %collective-permute-start.1 = (bf16[128,3584]{1,0:T(8,128)(2,1)}, bf16[128,3584]{1,0:T(8,128)(2,1)S(1)}, u32[]{:S(2)}, u32[]{:S(2)}) collective-permute-start(bf16[128,3584]{1,0:T(8,128)(2,1)} %collective-permute-done.refs_4_), channel_id=1, source_target_pairs={{0,64},{8,72},{16,80},{24,88},{32,96},{40,104},{48,112},{56,120},{... | collective-permute-start | bytes 2752520 | tf_op jit(solution)/shard_map/ppermute | solution.py:315
  25.2 26.9 %collective-permute-start.5 = (bf16[128,3584]{1,0:T(8,128)(2,1)}, bf16[128,3584]{1,0:T(8,128)(2,1)S(1)}, u32[]{:S(2)}, u32[]{:S(2)}) collective-permute-start(bf16[128,3584]{1,0:T(8,128)(2,1)} %collective-permute-done.4.refs_6_), channel_id=1, source_target_pairs={{0,48},{8,56},{16,0},{24,8},{32,16},{40,24},{48,32},{56,40},{64,11... | collective-permute-start | bytes 2752520 | tf_op jit(solution)/shard_map/ppermute | solution.py:315
  26.5 38.0 %collective-permute-start.11 = (bf16[128,3584]{1,0:T(8,128)(2,1)}, bf16[128,3584]{1,0:T(8,128)(2,1)}, u32[]{:S(2)}, u32[]{:S(2)}) collective-permute-start(bf16[128,3584]{1,0:T(8,128)(2,1)} %refs_0_.1), channel_id=1, source_target_pairs={{0,8},{8,0},{16,24},{24,16},{32,40},{40,32},{48,56},{56,48},{64,72... | collective-permute-start | bytes 2752520 | tf_op jit(solution)/shard_map/ppermute | solution.py:315
  30.5 22.7 %all-to-all-start = ((bf16[16,32,512]{2,1,0:T(8,128)(2,1)}), bf16[16,32,512]{2,1,0:T(8,128)(2,1)S(1)}, u32[]{:S(2)}, u32[]{:S(2)}) async-start(bf16[16,32,512]{2,1,0:T(8,128)(2,1)} %cut.1), calls=%async_computation | async-start | bytes 1048576 | tf_op jit(solution)/shard_map/all_to_all | solution.py:329
  49.6 5.2 %collective-permute-start.12 = (bf16[128,3584]{1,0:T(8,128)(2,1)}, bf16[128,3584]{1,0:T(8,128)(2,1)}, u32[]{:S(2)}, u32[]{:S(2)}) collective-permute-start(bf16[128,3584]{1,0:T(8,128)(2,1)} %collective-permute-done.refs_4_), channel_id=1, source_target_pairs={{0,8},{8,0},{16,24},{24,16},{32,40},{40,32},{48,56},{56,48},{64,72... | collective-permute-start | bytes 2752520 | tf_op jit(solution)/shard_map/ppermute | solution.py:315
  49.7 0.9 copy-start.4
  49.7 5.7 %collective-permute-start.15 = (bf16[128,3584]{1,0:T(8,128)(2,1)}, bf16[128,3584]{1,0:T(8,128)(2,1)}, u32[]{:S(2)}, u32[]{:S(2)}) collective-permute-start(bf16[128,3584]{1,0:T(8,128)(2,1)} %collective-permute-done.4.refs_6_), channel_id=1, source_target_pairs={{0,8},{8,0},{16,24},{24,16},{32,40},{40,32},{48,56},{56,48},{64,72... | collective-permute-start | bytes 2752520 | tf_op jit(solution)/shard_map/ppermute | solution.py:315
  50.6 22.8 %collective-permute-start.16 = (bf16[128,3584]{1,0:T(8,128)(2,1)}, bf16[128,3584]{1,0:T(8,128)(2,1)S(1)}, u32[]{:S(2)}, u32[]{:S(2)}) collective-permute-start(bf16[128,3584]{1,0:T(8,128)(2,1)} %collective-permute-done.refs_4_), channel_id=1, source_target_pairs={{0,16},{8,24},{16,32},{24,40},{32,48},{40,56},{48,0},{56,8},{64,80... | collective-permute-start | bytes 2752520 | tf_op jit(solution)/shard_map/ppermute | solution.py:315
  52.1 5.3 %collective-permute-start.14 = (bf16[128,3584]{1,0:T(8,128)(2,1)}, bf16[128,3584]{1,0:T(8,128)(2,1)}, u32[]{:S(2)}, u32[]{:S(2)}) collective-permute-start(bf16[128,3584]{1,0:T(8,128)(2,1)} %copy-done.4), channel_id=1, source_target_pairs={{0,8},{8,0},{16,24},{24,16},{32,40},{40,32},{48,56},{56,48},{64,72... | collective-permute-start | bytes 2752520 | tf_op jit(solution)/shard_map/ppermute | solution.py:315
  53.1 1.0 copy-start.3
  54.2 4.1 %copy-start = (bf16[3,3584,512]{2,1,0:T(8,128)(2,1)S(1)}, bf16[3,3584,512]{2,1,0:T(8,128)(2,1)}, u32[]{:S(2)}) copy-start(bf16[3,3584,512]{2,1,0:T(8,128)(2,1)} %early.1.refs_3_.refs_5_.refs_2_) | copy-start | bytes 33030148
  54.7 21.2 %copy-start.2 = (bf16[128,3584]{1,0:T(8,128)(2,1)S(1)}, bf16[128,3584]{1,0:T(8,128)(2,1)}, u32[]{:S(2)}) copy-start(bf16[128,3584]{1,0:T(8,128)(2,1)} %refs_0_.1) | copy-start | bytes 2752516
  54.7 34.1 %collective-permute-start.2 = (bf16[64,3584]{1,0:T(8,128)(2,1)S(1)}, bf16[64,3584]{1,0:T(8,128)(2,1)S(1)}, u32[]{:S(2)}, u32[]{:S(2)}) collective-permute-start(bf16[64,3584]{1,0:T(8,128)(2,1)S(1)} %slice.8), channel_id=1, source_target_pairs={{0,16},{8,24},{16,32},{24,40},{32,48},{40,56},{48,0},{56,8},{64,80... | collective-permute-start | bytes 1376264 | tf_op jit(solution)/shard_map/ppermute | solution.py:315
  55.4 34.7 %collective-permute-start.6 = (bf16[64,3584]{1,0:T(8,128)(2,1)S(1)}, bf16[64,3584]{1,0:T(8,128)(2,1)S(1)}, u32[]{:S(2)}, u32[]{:S(2)}) collective-permute-start(bf16[64,3584]{1,0:T(8,128)(2,1)S(1)} %slice.9), channel_id=1, source_target_pairs={{0,48},{8,56},{16,0},{24,8},{32,16},{40,24},{48,32},{56,40},{64,11... | collective-permute-start | bytes 1376264 | tf_op jit(solution)/shard_map/ppermute | solution.py:315
  57.5 34.1 %collective-permute-start.19 = (bf16[128,3584]{1,0:T(8,128)(2,1)S(1)}, bf16[128,3584]{1,0:T(8,128)(2,1)S(1)}, u32[]{:S(2)}, u32[]{:S(2)}) collective-permute-start(bf16[128,3584]{1,0:T(8,128)(2,1)S(1)} %collective-permute-done.1.refs_2_), channel_id=1, source_target_pairs={{0,8},{8,0},{16,24},{24,16},{32,40},{40,32},{48,56},{56,48},{64,72... | collective-permute-start | bytes 2752520 | tf_op jit(solution)/shard_map/ppermute | solution.py:315
  64.5 29.5 %collective-permute-start.18 = (bf16[128,3584]{1,0:T(8,128)(2,1)S(1)}, bf16[128,3584]{1,0:T(8,128)(2,1)S(1)}, u32[]{:S(2)}, u32[]{:S(2)}) collective-permute-start(bf16[128,3584]{1,0:T(8,128)(2,1)S(1)} %collective-permute-done.5.refs_1_), channel_id=1, source_target_pairs={{0,8},{8,0},{16,24},{24,16},{32,40},{40,32},{48,56},{56,48},{64,72... | collective-permute-start | bytes 2752520 | tf_op jit(solution)/shard_map/ppermute | solution.py:315
  73.4 19.7 %collective-permute-start.17 = (bf16[128,3584]{1,0:T(8,128)(2,1)S(1)}, bf16[128,3584]{1,0:T(8,128)(2,1)S(1)}, u32[]{:S(2)}, u32[]{:S(2)}) collective-permute-start(bf16[128,3584]{1,0:T(8,128)(2,1)S(1)} %collective-permute-done.16.refs_0_), channel_id=1, source_target_pairs={{0,8},{8,0},{16,24},{24,16},{32,40},{40,32},{48,56},{56,48},{64,72... | collective-permute-start | bytes 2752520 | tf_op jit(solution)/shard_map/ppermute | solution.py:315
  88.8 14.8 %collective-permute-start.10 = (bf16[16,32,512]{2,1,0:T(8,128)(2,1)S(1)}, bf16[16,32,512]{2,1,0:T(8,128)(2,1)S(1)}, u32[]{:S(2)}, u32[]{:S(2)}) collective-permute-start(bf16[16,32,512]{2,1,0:T(8,128)(2,1)S(1)} %turn.1.r0.refs_3_), channel_id=1, source_target_pairs={{0,1},{1,2},{2,3},{3,0},{4,5},{5,6},{6,7},{7,4},{8,9},{9,10},{10,1... | collective-permute-start | bytes 1572872 | tf_op jit(solution)/shard_map/ppermute | solution.py:315
  90.1 13.5 %collective-permute-start.8 = (bf16[16,32,512]{2,1,0:T(8,128)(2,1)S(1)}, bf16[16,32,512]{2,1,0:T(8,128)(2,1)S(1)}, u32[]{:S(2)}, u32[]{:S(2)}) collective-permute-start(bf16[16,32,512]{2,1,0:T(8,128)(2,1)S(1)} %turn.1.r0.refs_3_), channel_id=1, source_target_pairs={{0,3},{1,0},{2,1},{3,2},{4,7},{5,4},{6,5},{7,6},{8,11},{9,8},{10,9... | collective-permute-start | bytes 1572872 | tf_op jit(solution)/shard_map/ppermute | solution.py:315
  91.6 24.3 %collective-permute-start.9 = (bf16[16,32,512]{2,1,0:T(8,128)(2,1)S(1)}, bf16[16,32,512]{2,1,0:T(8,128)(2,1)S(1)}, u32[]{:S(2)}, u32[]{:S(2)}) collective-permute-start(bf16[16,32,512]{2,1,0:T(8,128)(2,1)S(1)} %turn.1.r0.refs_3_), channel_id=1, source_target_pairs={{0,2},{1,3},{2,0},{3,1},{4,6},{5,7},{6,4},{7,5},{8,10},{9,11},{10,... | collective-permute-start | bytes 1572872 | tf_op jit(solution)/shard_map/ppermute | solution.py:315
  93.2 25.3 %collective-permute-start.3 = (bf16[64,3584]{1,0:T(8,128)(2,1)S(1)}, bf16[64,3584]{1,0:T(8,128)(2,1)S(1)}, u32[]{:S(2)}, u32[]{:S(2)}) collective-permute-start(bf16[64,3584]{1,0:T(8,128)(2,1)S(1)} %collective-permute-done.2.refs_0_), channel_id=1, source_target_pairs={{0,8},{8,0},{16,24},{24,16},{32,40},{40,32},{48,56},{56,48},{64,72... | collective-permute-start | bytes 1376264 | tf_op jit(solution)/shard_map/ppermute | solution.py:315
  94.0 24.5 %collective-permute-start.7 = (bf16[64,3584]{1,0:T(8,128)(2,1)S(1)}, bf16[64,3584]{1,0:T(8,128)(2,1)S(1)}, u32[]{:S(2)}, u32[]{:S(2)}) collective-permute-start(bf16[64,3584]{1,0:T(8,128)(2,1)S(1)} %collective-permute-done.6.refs_1_), channel_id=1, source_target_pairs={{0,8},{8,0},{16,24},{24,16},{32,40},{40,32},{48,56},{56,48},{64,72... | collective-permute-start | bytes 1376264 | tf_op jit(solution)/shard_map/ppermute | solution.py:315
  95.9 20.0 %copy-start.1 = (s32[2048]{0:T(1024)S(1)}, s32[2048]{0:T(1024)}, u32[]{:S(2)}) copy-start(s32[2048]{0:T(1024)} %param.13) | copy-start | bytes 24580

commit v3 on v2

--- a/solution.py
+++ b/solution.py
@@ -101,7 +101,7 @@
         cost_estimate=pl.CostEstimate(flops=4 * 10**10, bytes_accessed=3 << 19, transcendentals=0),
         compiler_params=pltpu.CompilerParams(vmem_limit_bytes=8 << 20),
         name="turn",
-    )(dp, rows, basis)
+    )(dp, rows, distant(basis))
 
 
 def folded(basis_ref, query_ref, eigen_ref):
@@ -125,21 +125,22 @@
     )
 
 
-def early_kernel(basis_ref, query_ref, eigen_ref, out_ref):
+def fold_kernel(basis_ref, query_ref, eigen_ref, *refs):
     for q, values in folded(basis_ref, query_ref, eigen_ref):
-        out_ref[q] = values
-
-
-def fold_early(nblocks, basis_out, query, eigenvalues):
-    return pl.pallas_call(
-        early_kernel,
-        out_shape=jax.ShapeDtypeStruct((Q, nblocks * BLK, BLK), BF16),
-        grid=(nblocks,),
-        in_specs=fold_specs(0),
-        out_specs=pl.BlockSpec((Q, BLK, BLK), lambda b: (0, b, 0)),
-        cost_estimate=fold_cost(nblocks),
-        name="early",
-    )(distant(basis_out), distant(query), distant(eigenvalues))
+        refs[-1][q] = values
+
+
+def fold(first, last, basis_out, query, eigenvalues, partial=None):
+    extra = [] if partial is None else [partial]
+    return pl.pallas_call(
+        fold_kernel,
+        out_shape=jax.ShapeDtypeStruct(query.shape, BF16),
+        grid=(last - first,),
+        in_specs=fold_specs(first) + [pl.BlockSpec(memory_space=pltpu.HBM)] * len(extra),
+        out_specs=pl.BlockSpec((Q, BLK, BLK), lambda b: (0, first + b, 0)),
+        input_output_aliases={3: 0} if extra else {},
+        cost_estimate=fold_cost(last - first),
+    )(distant(basis_out), distant(query), distant(eigenvalues), *[distant(v) for v in extra])
 
 
 TILE = 256
@@ -332,7 +333,7 @@
     pieces = [pieces[0], pieces[1], pieces[3], pieces[2]]
 
     query = jnp.transpose(query_grads, (1, 0, 2))
-    weight = fold_early(7, basis_out, query, eigenvalues)
+    weight = fold(0, basis_out.shape[0], basis_out, query, eigenvalues)
 
     a2 = move(a3, RIGHT)
     b3 = move(a3, ACROSS)

time: 140 us -> 140 us (level)
  local copies, waits for them, and re-layouts: 2.03 us -> 0.62 us
    unnamed x10 -> x8, local copies, waits for them, and re-layouts: 1.96 us -> 0.55 us
where the time goes in v3:
time: 140 us; the launch traced here: 139 us
  Pallas kernels  50 us (36%)
  waiting for transfers between devices  43.4 us (31%)
  starting transfers between devices  27.6 us (20%)
  blocking collectives  17.3 us (12%)
    ppermute x20, waiting for transfers between devices, move(): return lax.ppermute(v, axis, perm)  42.9 us
    pallas_call x5, Pallas kernels, product(): pl.pallas_call(functools.partial(product_kernel, len(rows)), out_shape=(p...  25 us
    ppermute x20, starting transfers between devices, move(): return lax.ppermute(v, axis, perm)  24.1 us
    all_to_all x1, blocking collectives, on_device(): partials = lax.all_to_all(partial, ('dp', 'group'), 0, 0, tiled=True)  17.3 us
    pallas_call x1, Pallas kernels, fold(): pl.pallas_call(fold_kernel, out_shape=jax.ShapeDtypeStruct(query.shape, B...  15.5 us
    all_to_all x1, starting transfers between devices, on_device(): lax.all_to_all(cut(activations, position[1:]), 'dp', 0, 0, tiled=True)  3.47 us
  transfers between devices with their start and end apart: 21, of which 5 were waited for; matrix products, arithmetic and copies ran while one was open for 0% of the time, Pallas kernels for 33%

profile of v3, /device:TPU:1, one launch (start us, length us, event | category | flops | bytes accessed | tf_op | source)
XLA Modules:
  0.0 139.2 jit_solution(11545189340590328703)
XLA Ops:
  0.0 2.0 %collective-permute-start = (bf16[128,3584]{1,0:T(8,128)(2,1)}, bf16[128,3584]{1,0:T(8,128)(2,1)}, u32[]{:S(2)}, u32[]{:S(2)}) collective-permute-start(bf16[128,3584]{1,0:T(8,128)(2,1)} %refs_0_.1), channel_id=1, source_target_pairs={{0,16},{8,24},{16,32},{24,40},{32,48},{40,56},{48,0},{56,8},{64,80... | collective-permute-start | bytes 2752520 | tf_op jit(solution)/shard_map/ppermute | solution.py:316
  2.0 1.6 %collective-permute-start.4 = (bf16[128,3584]{1,0:T(8,128)(2,1)}, bf16[128,3584]{1,0:T(8,128)(2,1)}, u32[]{:S(2)}, u32[]{:S(2)}) collective-permute-start(bf16[128,3584]{1,0:T(8,128)(2,1)} %refs_0_.1), channel_id=1, source_target_pairs={{0,64},{8,72},{16,80},{24,88},{32,96},{40,104},{48,112},{56,120},{... | collective-permute-start | bytes 2752520 | tf_op jit(solution)/shard_map/ppermute | solution.py:316
  3.7 1.5 %collective-permute-start.13 = (bf16[128,3584]{1,0:T(8,128)(2,1)}, bf16[128,3584]{1,0:T(8,128)(2,1)S(1)}, u32[]{:S(2)}, u32[]{:S(2)}) collective-permute-start(bf16[128,3584]{1,0:T(8,128)(2,1)} %refs_0_.1), channel_id=1, source_target_pairs={{0,48},{8,56},{16,0},{24,8},{32,16},{40,24},{48,32},{56,40},{64,11... | collective-permute-start | bytes 2752520 | tf_op jit(solution)/shard_map/ppermute | solution.py:316
  5.1 18.2 %collective-permute-done.refs_4_ = bf16[128,3584]{1,0:T(8,128)(2,1)} collective-permute-done((bf16[128,3584]{1,0:T(8,128)(2,1)}, bf16[128,3584]{1,0:T(8,128)(2,1)}, u32[]{:S(2)}, u32[]{:S(2)}) %collective-permute-start) | collective-permute-done | bytes 917536 | tf_op jit(solution)/shard_map/ppermute | solution.py:316
  23.3 1.9 %collective-permute-start.1 = (bf16[128,3584]{1,0:T(8,128)(2,1)}, bf16[128,3584]{1,0:T(8,128)(2,1)S(1)}, u32[]{:S(2)}, u32[]{:S(2)}) collective-permute-start(bf16[128,3584]{1,0:T(8,128)(2,1)} %collective-permute-done.refs_4_), channel_id=1, source_target_pairs={{0,64},{8,72},{16,80},{24,88},{32,96},{40,104},{48,112},{56,120},{... | collective-permute-start | bytes 2752520 | tf_op jit(solution)/shard_map/ppermute | solution.py:316
  25.2 1.3 collective-permute-start.5
  26.5 2.1 %collective-permute-start.11 = (bf16[128,3584]{1,0:T(8,128)(2,1)}, bf16[128,3584]{1,0:T(8,128)(2,1)}, u32[]{:S(2)}, u32[]{:S(2)}) collective-permute-start(bf16[128,3584]{1,0:T(8,128)(2,1)} %refs_0_.1), channel_id=1, source_target_pairs={{0,8},{8,0},{16,24},{24,16},{32,40},{40,32},{48,56},{56,48},{64,72... | collective-permute-start | bytes 2752520 | tf_op jit(solution)/shard_map/ppermute | solution.py:316
  28.6 1.9 %cut.1 = bf16[16,32,512]{2,1,0:T(8,128)(2,1)} custom-call(s32[1]{0:T(128)} %bitcast.1.y_ref, bf16[128,8192]{1,0:T(8,128)(2,1)} %rows_ref.1), custom_call_target="tpu_custom_call" | custom-call | bytes 1048576 | tf_op jit(solution)/shard_map/cut/pallas_call | solution.py:63
  30.5 3.5 %all-to-all-start = ((bf16[16,32,512]{2,1,0:T(8,128)(2,1)}), bf16[16,32,512]{2,1,0:T(8,128)(2,1)S(1)}, u32[]{:S(2)}, u32[]{:S(2)}) async-start(bf16[16,32,512]{2,1,0:T(8,128)(2,1)} %cut.1), calls=%async_computation | async-start | bytes 1048576 | tf_op jit(solution)/shard_map/all_to_all | solution.py:330
  34.0 15.5 %shard_map.73.refs_3_.refs_5_.refs_2_ = bf16[3,3584,512]{2,1,0:T(8,128)(2,1)} custom-call(bf16[7,512,512]{2,1,0:T(8,128)(2,1)} %basis_ref.2, bf16[3,3584,512]{2,1,0:T(8,128)(2,1)} %bitcast.6, bf16[3584,512]{1,0:T(8,128)(2,1)} %eigen_ref.1), custom_call_target="tpu_custom_call" | custom-call | flops 5637144576 | bytes 29360128 | tf_op jit(solution)/shard_map/pallas_call | solution.py:135
  50.6 1.5 %collective-permute-start.16 = (bf16[128,3584]{1,0:T(8,128)(2,1)}, bf16[128,3584]{1,0:T(8,128)(2,1)S(1)}, u32[]{:S(2)}, u32[]{:S(2)}) collective-permute-start(bf16[128,3584]{1,0:T(8,128)(2,1)} %collective-permute-done.refs_4_), channel_id=1, source_target_pairs={{0,16},{8,24},{16,32},{24,40},{32,48},{40,56},{48,0},{56,8},{64,80... | collective-permute-start | bytes 2752520 | tf_op jit(solution)/shard_map/ppermute | solution.py:316
  52.5 0.6 all-to-all-done.rows_ref
  53.1 1.6 %turn.1.r0.refs_3_ = bf16[16,32,512]{2,1,0:T(8,128)(2,1)S(1)} custom-call(s32[1]{0:T(128)} %bitcast.dp_ref, bf16[16,32,512]{2,1,0:T(8,128)(2,1)S(1)} %all-to-all-done.rows_ref, bf16[1,512,512]{2,1,0:T(8,128)(2,1)} %basis_ref.3), custom_call_target="tpu_custom_call" | custom-call | flops 40000000000 | bytes 1572864 | tf_op jit(solution)/shard_map/turn/pallas_call | solution.py:88
  54.9 0.7 collective-permute-start.2
  55.6 2.1 %collective-permute-start.6 = (bf16[64,3584]{1,0:T(8,128)(2,1)S(1)}, bf16[64,3584]{1,0:T(8,128)(2,1)S(1)}, u32[]{:S(2)}, u32[]{:S(2)}) collective-permute-start(bf16[64,3584]{1,0:T(8,128)(2,1)S(1)} %slice.9), channel_id=1, source_target_pairs={{0,48},{8,56},{16,0},{24,8},{32,16},{40,24},{48,32},{56,40},{64,11... | collective-permute-start | bytes 1376264 | tf_op jit(solution)/shard_map/ppermute | solution.py:316
  58.1 6.2 %shard_map.74 = (f32[3,384,512]{2,1,0:T(8,128)S(1)}, bf16[128,3584]{1,0:T(8,128)(2,1)S(1)}, bf16[128,3584]{1,0:T(8,128)(2,1)S(1)}, bf16[128,3584]{1,0:T(8,128)(2,1)S(1)}) custom-call(bf16[128,3584]{1,0:T(8,128)(2,1)} %collective-permute-done.12.refs_0_, bf16[128,3584]{1,0:T(8,128)(2,1)} %collective-permute-done.14.refs_1_, ...), custom_call_target="tpu_custom_call" | custom-call | flops 4227858432 | tf_op jit(solution)/shard_map/pallas_call | solution.py:177
  64.4 9.1 %collective-permute-done.16.refs_0_ = bf16[128,3584]{1,0:T(8,128)(2,1)S(1)} collective-permute-done((bf16[128,3584]{1,0:T(8,128)(2,1)}, bf16[128,3584]{1,0:T(8,128)(2,1)S(1)}, u32[]{:S(2)}, u32[]{:S(2)}) %collective-permute-start.16) | collective-permute-done | bytes 917536 | tf_op jit(solution)/shard_map/ppermute | solution.py:316
  73.5 2.5 %collective-permute-start.17 = (bf16[128,3584]{1,0:T(8,128)(2,1)S(1)}, bf16[128,3584]{1,0:T(8,128)(2,1)S(1)}, u32[]{:S(2)}, u32[]{:S(2)}) collective-permute-start(bf16[128,3584]{1,0:T(8,128)(2,1)S(1)} %collective-permute-done.16.refs_0_), channel_id=1, source_target_pairs={{0,8},{8,0},{16,24},{24,16},{32,40},{40,32},{48,56},{56,48},{64,72... | collective-permute-start | bytes 2752520 | tf_op jit(solution)/shard_map/ppermute | solution.py:316
  75.9 8.4 %shard_map.75.refs_0_ = f32[3,640,512]{2,1,0:T(8,128)S(1)} custom-call(bf16[128,3584]{1,0:T(8,128)(2,1)S(1)} %copy-done.2, bf16[128,3584]{1,0:T(8,128)(2,1)} %collective-permute-done.11.refs_1_, bf16[128,3584]{1,0:T(8,128)(2,1)S(1)} %get-tuple-element.9.refs_2_, bf16[128,3584]{1,0:T(8,128)(2,1)S(1)} %get-tuple-element.10.refs_3_, ...), custom_call_target="tpu_custom_call" | custom-call | flops 7046430720 | tf_op jit(solution)/shard_map/pallas_call | solution.py:177
  84.4 4.4 %shard_map.76.refs_2_ = f32[3,384,512]{2,1,0:T(8,128)S(1)} custom-call(bf16[128,3584]{1,0:T(8,128)(2,1)S(1)} %collective-permute-done.16.refs_0_, bf16[128,3584]{1,0:T(8,128)(2,1)S(1)} %collective-permute-done.5.refs_1_, bf16[128,3584]{1,0:T(8,128)(2,1)S(1)} %collective-permute-done.1.refs_2_, bf16[3,3584,512]{2,1,0:T(8,128)(2,1)S(1)} %copy-done), custom_call_target="tpu_custom_call" | custom-call | flops 4227858432 | tf_op jit(solution)/shard_map/pallas_call | solution.py:177
  88.8 1.3 collective-permute-start.10
  90.1 1.5 %collective-permute-start.8 = (bf16[16,32,512]{2,1,0:T(8,128)(2,1)S(1)}, bf16[16,32,512]{2,1,0:T(8,128)(2,1)S(1)}, u32[]{:S(2)}, u32[]{:S(2)}) collective-permute-start(bf16[16,32,512]{2,1,0:T(8,128)(2,1)S(1)} %turn.1.r0.refs_3_), channel_id=1, source_target_pairs={{0,3},{1,0},{2,1},{3,2},{4,7},{5,4},{6,5},{7,6},{8,11},{9,8},{10,9... | collective-permute-start | bytes 1572872 | tf_op jit(solution)/shard_map/ppermute | solution.py:316
  91.6 1.6 %collective-permute-start.9 = (bf16[16,32,512]{2,1,0:T(8,128)(2,1)S(1)}, bf16[16,32,512]{2,1,0:T(8,128)(2,1)S(1)}, u32[]{:S(2)}, u32[]{:S(2)}) collective-permute-start(bf16[16,32,512]{2,1,0:T(8,128)(2,1)S(1)} %turn.1.r0.refs_3_), channel_id=1, source_target_pairs={{0,2},{1,3},{2,0},{3,1},{4,6},{5,7},{6,4},{7,5},{8,10},{9,11},{10,... | collective-permute-start | bytes 1572872 | tf_op jit(solution)/shard_map/ppermute | solution.py:316
  93.2 0.8 collective-permute-start.3
  94.3 1.6 %shard_map.79.refs_9_ = f32[3,128,512]{2,1,0:T(8,128)S(1)} custom-call(bf16[64,3584]{1,0:T(8,128)(2,1)S(1)} %collective-permute-done.2.refs_0_, bf16[64,3584]{1,0:T(8,128)(2,1)S(1)} %collective-permute-done.6.refs_1_, bf16[3,3584,512]{2,1,0:T(8,128)(2,1)S(1)} %copy-done), custom_call_target="tpu_custom_call" | custom-call | flops 1409286144 | tf_op jit(solution)/shard_map/pallas_call | solution.py:177
  95.9 4.4 %shard_map.77.refs_3_ = f32[3,384,512]{2,1,0:T(8,128)S(1)} custom-call(bf16[128,3584]{1,0:T(8,128)(2,1)S(1)} %collective-permute-done.17.refs_0_, bf16[128,3584]{1,0:T(8,128)(2,1)S(1)} %collective-permute-done.18.refs_1_, bf16[128,3584]{1,0:T(8,128)(2,1)S(1)} %collective-permute-done.19.refs_2_, bf16[3,3584,512]{2,1,0:T(8,128)(2,1)S(1)} %copy-done), custom_call_target="tpu_custom_call" | custom-call | flops 4227858432 | tf_op jit(solution)/shard_map/pallas_call | solution.py:177
  100.3 3.2 %collective-permute-done.10.r3.refs_6_ = bf16[16,32,512]{2,1,0:T(8,128)(2,1)S(1)} collective-permute-done((bf16[16,32,512]{2,1,0:T(8,128)(2,1)S(1)}, bf16[16,32,512]{2,1,0:T(8,128)(2,1)S(1)}, u32[]{:S(2)}, u32[]{:S(2)}) %collective-permute-start.10) | collective-permute-done | bytes 524320 | tf_op jit(solution)/shard_map/ppermute | solution.py:316
  103.6 12.4 %collective-permute-done.9.r2.refs_5_ = bf16[16,32,512]{2,1,0:T(8,128)(2,1)S(1)} collective-permute-done((bf16[16,32,512]{2,1,0:T(8,128)(2,1)S(1)}, bf16[16,32,512]{2,1,0:T(8,128)(2,1)S(1)}, u32[]{:S(2)}, u32[]{:S(2)}) %collective-permute-start.9) | collective-permute-done | bytes 524320 | tf_op jit(solution)/shard_map/ppermute | solution.py:316
  115.9 2.5 %shard_map.78.refs_8_ = f32[64,384]{1,0:T(8,128)S(1)} custom-call(s32[2]{0:T(128)S(1)} %pad_add_fusion.pos_ref, bf16[16,32,512]{2,1,0:T(8,128)(2,1)S(1)} %turn.1.r0.refs_3_, bf16[16,32,512]{2,1,0:T(8,128)(2,1)S(1)} %collective-permute-done.8.r1.refs_4_, bf16[16,32,512]{2,1,0:T(8,128)(2,1)S(1)} %collective-permute-done.9.r2.refs_5_, ...), custom_call_target="tpu_custom_call" | custom-call | flops 5505024 | bytes 8388608 | tf_op jit(solution)/shard_map/pallas_call | solution.py:242
  118.5 2.7 %shard_map.80 = f32[128,1,192]{2,1,0:T(1,128)S(1)} custom-call(s32[2]{0:T(128)S(1)} %pad_add_fusion.pos_ref, bf16[64,3584]{1,0:T(8,128)(2,1)S(1)} %collective-permute-done.3.refs_0_, bf16[64,3584]{1,0:T(8,128)(2,1)S(1)} %collective-permute-done.7.refs_1_, bf16[3,3584,512]{2,1,0:T(8,128)(2,1)S(1)} %copy-done, bf16[16,32,512]{2,1,0:T(8,128)(2,1)S(1)} %turn.1.r0.refs_3_, ...), custom_call_target="tpu_custom_call" | custom-call | flops 2818572288 | tf_op jit(solution)/shard_map/pallas_call | solution.py:288
  121.2 17.3 %all_to_all.10.parts_ref = f32[128,1,192]{2,1,0:T(1,128)S(1)} all-to-all(f32[128,1,192]{2,1,0:T(1,128)S(1)} %shard_map.80), channel_id=1, replica_groups=mesh['dp'=16,'group'=8] {'dp','group'}, dimensions={0} | all-to-all | bytes 196608 | tf_op jit(solution)/shard_map/all_to_all | solution.py:357
  138.4 0.8 finish.1
  (33 shorter events, 2.5 us)
Async XLA Ops:
  0.0 23.3 %collective-permute-start = (bf16[128,3584]{1,0:T(8,128)(2,1)}, bf16[128,3584]{1,0:T(8,128)(2,1)}, u32[]{:S(2)}, u32[]{:S(2)}) collective-permute-start(bf16[128,3584]{1,0:T(8,128)(2,1)} %refs_0_.1), channel_id=1, source_target_pairs={{0,16},{8,24},{16,32},{24,40},{32,48},{40,56},{48,0},{56,8},{64,80... | collective-permute-start | bytes 2752520 | tf_op jit(solution)/shard_map/ppermute | solution.py:316
  2.0 23.2 %collective-permute-start.4 = (bf16[128,3584]{1,0:T(8,128)(2,1)}, bf16[128,3584]{1,0:T(8,128)(2,1)}, u32[]{:S(2)}, u32[]{:S(2)}) collective-permute-start(bf16[128,3584]{1,0:T(8,128)(2,1)} %refs_0_.1), channel_id=1, source_target_pairs={{0,64},{8,72},{16,80},{24,88},{32,96},{40,104},{48,112},{56,120},{... | collective-permute-start | bytes 2752520 | tf_op jit(solution)/shard_map/ppermute | solution.py:316
  3.7 46.0 %collective-permute-start.13 = (bf16[128,3584]{1,0:T(8,128)(2,1)}, bf16[128,3584]{1,0:T(8,128)(2,1)S(1)}, u32[]{:S(2)}, u32[]{:S(2)}) collective-permute-start(bf16[128,3584]{1,0:T(8,128)(2,1)} %refs_0_.1), channel_id=1, source_target_pairs={{0,48},{8,56},{16,0},{24,8},{32,16},{40,24},{48,32},{56,40},{64,11... | collective-permute-start | bytes 2752520 | tf_op jit(solution)/shard_map/ppermute | solution.py:316
  23.3 27.3 %collective-permute-start.1 = (bf16[128,3584]{1,0:T(8,128)(2,1)}, bf16[128,3584]{1,0:T(8,128)(2,1)S(1)}, u32[]{:S(2)}, u32[]{:S(2)}) collective-permute-start(bf16[128,3584]{1,0:T(8,128)(2,1)} %collective-permute-done.refs_4_), channel_id=1, source_target_pairs={{0,64},{8,72},{16,80},{24,88},{32,96},{40,104},{48,112},{56,120},{... | collective-permute-start | bytes 2752520 | tf_op jit(solution)/shard_map/ppermute | solution.py:316
  25.2 26.9 %collective-permute-start.5 = (bf16[128,3584]{1,0:T(8,128)(2,1)}, bf16[128,3584]{1,0:T(8,128)(2,1)S(1)}, u32[]{:S(2)}, u32[]{:S(2)}) collective-permute-start(bf16[128,3584]{1,0:T(8,128)(2,1)} %collective-permute-done.4.refs_6_), channel_id=1, source_target_pairs={{0,48},{8,56},{16,0},{24,8},{32,16},{40,24},{48,32},{56,40},{64,11... | collective-permute-start | bytes 2752520 | tf_op jit(solution)/shard_map/ppermute | solution.py:316
  26.5 37.8 %collective-permute-start.11 = (bf16[128,3584]{1,0:T(8,128)(2,1)}, bf16[128,3584]{1,0:T(8,128)(2,1)}, u32[]{:S(2)}, u32[]{:S(2)}) collective-permute-start(bf16[128,3584]{1,0:T(8,128)(2,1)} %refs_0_.1), channel_id=1, source_target_pairs={{0,8},{8,0},{16,24},{24,16},{32,40},{40,32},{48,56},{56,48},{64,72... | collective-permute-start | bytes 2752520 | tf_op jit(solution)/shard_map/ppermute | solution.py:316
  30.5 22.7 %all-to-all-start = ((bf16[16,32,512]{2,1,0:T(8,128)(2,1)}), bf16[16,32,512]{2,1,0:T(8,128)(2,1)S(1)}, u32[]{:S(2)}, u32[]{:S(2)}) async-start(bf16[16,32,512]{2,1,0:T(8,128)(2,1)} %cut.1), calls=%async_computation | async-start | bytes 1048576 | tf_op jit(solution)/shard_map/all_to_all | solution.py:330
  49.6 5.3 %collective-permute-start.12 = (bf16[128,3584]{1,0:T(8,128)(2,1)}, bf16[128,3584]{1,0:T(8,128)(2,1)}, u32[]{:S(2)}, u32[]{:S(2)}) collective-permute-start(bf16[128,3584]{1,0:T(8,128)(2,1)} %collective-permute-done.refs_4_), channel_id=1, source_target_pairs={{0,8},{8,0},{16,24},{24,16},{32,40},{40,32},{48,56},{56,48},{64,72... | collective-permute-start | bytes 2752520 | tf_op jit(solution)/shard_map/ppermute | solution.py:316
  49.7 0.9 copy-start.3
  49.7 5.9 %collective-permute-start.15 = (bf16[128,3584]{1,0:T(8,128)(2,1)}, bf16[128,3584]{1,0:T(8,128)(2,1)}, u32[]{:S(2)}, u32[]{:S(2)}) collective-permute-start(bf16[128,3584]{1,0:T(8,128)(2,1)} %collective-permute-done.4.refs_6_), channel_id=1, source_target_pairs={{0,8},{8,0},{16,24},{24,16},{32,40},{40,32},{48,56},{56,48},{64,72... | collective-permute-start | bytes 2752520 | tf_op jit(solution)/shard_map/ppermute | solution.py:316
  50.6 22.9 %collective-permute-start.16 = (bf16[128,3584]{1,0:T(8,128)(2,1)}, bf16[128,3584]{1,0:T(8,128)(2,1)S(1)}, u32[]{:S(2)}, u32[]{:S(2)}) collective-permute-start(bf16[128,3584]{1,0:T(8,128)(2,1)} %collective-permute-done.refs_4_), channel_id=1, source_target_pairs={{0,16},{8,24},{16,32},{24,40},{32,48},{40,56},{48,0},{56,8},{64,80... | collective-permute-start | bytes 2752520 | tf_op jit(solution)/shard_map/ppermute | solution.py:316
  52.1 5.5 %collective-permute-start.14 = (bf16[128,3584]{1,0:T(8,128)(2,1)}, bf16[128,3584]{1,0:T(8,128)(2,1)}, u32[]{:S(2)}, u32[]{:S(2)}) collective-permute-start(bf16[128,3584]{1,0:T(8,128)(2,1)} %copy-done.3), channel_id=1, source_target_pairs={{0,8},{8,0},{16,24},{24,16},{32,40},{40,32},{48,56},{56,48},{64,72... | collective-permute-start | bytes 2752520 | tf_op jit(solution)/shard_map/ppermute | solution.py:316
  53.1 4.9 %copy-start = (bf16[3,3584,512]{2,1,0:T(8,128)(2,1)S(1)}, bf16[3,3584,512]{2,1,0:T(8,128)(2,1)}, u32[]{:S(2)}) copy-start(bf16[3,3584,512]{2,1,0:T(8,128)(2,1)} %shard_map.73.refs_3_.refs_5_.refs_2_) | copy-start | bytes 33030148
  54.8 21.1 %copy-start.2 = (bf16[128,3584]{1,0:T(8,128)(2,1)S(1)}, bf16[128,3584]{1,0:T(8,128)(2,1)}, u32[]{:S(2)}) copy-start(bf16[128,3584]{1,0:T(8,128)(2,1)} %refs_0_.1) | copy-start | bytes 2752516
  54.9 33.9 %collective-permute-start.2 = (bf16[64,3584]{1,0:T(8,128)(2,1)S(1)}, bf16[64,3584]{1,0:T(8,128)(2,1)S(1)}, u32[]{:S(2)}, u32[]{:S(2)}) collective-permute-start(bf16[64,3584]{1,0:T(8,128)(2,1)S(1)} %slice.8), channel_id=1, source_target_pairs={{0,16},{8,24},{16,32},{24,40},{32,48},{40,56},{48,0},{56,8},{64,80... | collective-permute-start | bytes 1376264 | tf_op jit(solution)/shard_map/ppermute | solution.py:316
  55.6 34.5 %collective-permute-start.6 = (bf16[64,3584]{1,0:T(8,128)(2,1)S(1)}, bf16[64,3584]{1,0:T(8,128)(2,1)S(1)}, u32[]{:S(2)}, u32[]{:S(2)}) collective-permute-start(bf16[64,3584]{1,0:T(8,128)(2,1)S(1)} %slice.9), channel_id=1, source_target_pairs={{0,48},{8,56},{16,0},{24,8},{32,16},{40,24},{48,32},{56,40},{64,11... | collective-permute-start | bytes 1376264 | tf_op jit(solution)/shard_map/ppermute | solution.py:316
  57.6 34.0 %collective-permute-start.19 = (bf16[128,3584]{1,0:T(8,128)(2,1)S(1)}, bf16[128,3584]{1,0:T(8,128)(2,1)S(1)}, u32[]{:S(2)}, u32[]{:S(2)}) collective-permute-start(bf16[128,3584]{1,0:T(8,128)(2,1)S(1)} %collective-permute-done.1.refs_2_), channel_id=1, source_target_pairs={{0,8},{8,0},{16,24},{24,16},{32,40},{40,32},{48,56},{56,48},{64,72... | collective-permute-start | bytes 2752520 | tf_op jit(solution)/shard_map/ppermute | solution.py:316
  64.3 29.7 %collective-permute-start.18 = (bf16[128,3584]{1,0:T(8,128)(2,1)S(1)}, bf16[128,3584]{1,0:T(8,128)(2,1)S(1)}, u32[]{:S(2)}, u32[]{:S(2)}) collective-permute-start(bf16[128,3584]{1,0:T(8,128)(2,1)S(1)} %collective-permute-done.5.refs_1_), channel_id=1, source_target_pairs={{0,8},{8,0},{16,24},{24,16},{32,40},{40,32},{48,56},{56,48},{64,72... | collective-permute-start | bytes 2752520 | tf_op jit(solution)/shard_map/ppermute | solution.py:316
  73.5 19.7 %collective-permute-start.17 = (bf16[128,3584]{1,0:T(8,128)(2,1)S(1)}, bf16[128,3584]{1,0:T(8,128)(2,1)S(1)}, u32[]{:S(2)}, u32[]{:S(2)}) collective-permute-start(bf16[128,3584]{1,0:T(8,128)(2,1)S(1)} %collective-permute-done.16.refs_0_), channel_id=1, source_target_pairs={{0,8},{8,0},{16,24},{24,16},{32,40},{40,32},{48,56},{56,48},{64,72... | collective-permute-start | bytes 2752520 | tf_op jit(solution)/shard_map/ppermute | solution.py:316
  88.8 14.8 %collective-permute-start.10 = (bf16[16,32,512]{2,1,0:T(8,128)(2,1)S(1)}, bf16[16,32,512]{2,1,0:T(8,128)(2,1)S(1)}, u32[]{:S(2)}, u32[]{:S(2)}) collective-permute-start(bf16[16,32,512]{2,1,0:T(8,128)(2,1)S(1)} %turn.1.r0.refs_3_), channel_id=1, source_target_pairs={{0,1},{1,2},{2,3},{3,0},{4,5},{5,6},{6,7},{7,4},{8,9},{9,10},{10,1... | collective-permute-start | bytes 1572872 | tf_op jit(solution)/shard_map/ppermute | solution.py:316
  90.1 13.5 %collective-permute-start.8 = (bf16[16,32,512]{2,1,0:T(8,128)(2,1)S(1)}, bf16[16,32,512]{2,1,0:T(8,128)(2,1)S(1)}, u32[]{:S(2)}, u32[]{:S(2)}) collective-permute-start(bf16[16,32,512]{2,1,0:T(8,128)(2,1)S(1)} %turn.1.r0.refs_3_), channel_id=1, source_target_pairs={{0,3},{1,0},{2,1},{3,2},{4,7},{5,4},{6,5},{7,6},{8,11},{9,8},{10,9... | collective-permute-start | bytes 1572872 | tf_op jit(solution)/shard_map/ppermute | solution.py:316
  91.6 24.3 %collective-permute-start.9 = (bf16[16,32,512]{2,1,0:T(8,128)(2,1)S(1)}, bf16[16,32,512]{2,1,0:T(8,128)(2,1)S(1)}, u32[]{:S(2)}, u32[]{:S(2)}) collective-permute-start(bf16[16,32,512]{2,1,0:T(8,128)(2,1)S(1)} %turn.1.r0.refs_3_), channel_id=1, source_target_pairs={{0,2},{1,3},{2,0},{3,1},{4,6},{5,7},{6,4},{7,5},{8,10},{9,11},{10,... | collective-permute-start | bytes 1572872 | tf_op jit(solution)/shard_map/ppermute | solution.py:316
  93.2 25.3 %collective-permute-start.3 = (bf16[64,3584]{1,0:T(8,128)(2,1)S(1)}, bf16[64,3584]{1,0:T(8,128)(2,1)S(1)}, u32[]{:S(2)}, u32[]{:S(2)}) collective-permute-start(bf16[64,3584]{1,0:T(8,128)(2,1)S(1)} %collective-permute-done.2.refs_0_), channel_id=1, source_target_pairs={{0,8},{8,0},{16,24},{24,16},{32,40},{40,32},{48,56},{56,48},{64,72... | collective-permute-start | bytes 1376264 | tf_op jit(solution)/shard_map/ppermute | solution.py:316
  94.0 24.5 %collective-permute-start.7 = (bf16[64,3584]{1,0:T(8,128)(2,1)S(1)}, bf16[64,3584]{1,0:T(8,128)(2,1)S(1)}, u32[]{:S(2)}, u32[]{:S(2)}) collective-permute-start(bf16[64,3584]{1,0:T(8,128)(2,1)S(1)} %collective-permute-done.6.refs_1_), channel_id=1, source_target_pairs={{0,8},{8,0},{16,24},{24,16},{32,40},{40,32},{48,56},{56,48},{64,72... | collective-permute-start | bytes 1376264 | tf_op jit(solution)/shard_map/ppermute | solution.py:316
  95.9 20.0 %copy-start.1 = (s32[2048]{0:T(1024)S(1)}, s32[2048]{0:T(1024)}, u32[]{:S(2)}) copy-start(s32[2048]{0:T(1024)} %param.13) | copy-start | bytes 24580
